TPU v7x, 32 devices: a whole 2x2x4 slice. The times are simulated.
32 devices in a mesh: dp: 16 (over z, x, core), frame: 2 (over y).
Axes of the slice: x: 2, y: 2, z: 4, core: 2. Of those that a mesh axis runs over, the one named last changes fastest.
Arguments:
- video_tokens: bfloat16 [256, 2, 32, 1024], P('dp', 'frame'), may hold values from -14 to 14
- pool_weight: bfloat16 [2, 16, 32], P('frame'), may hold values from -1 to 1
- text_states: bfloat16 [256, 77, 1600], P(('dp', 'frame')), may hold values from -6 to 6
- norm_gain: float32 [1600], replicated, may hold values from 0.5 to 1.5
- lengths: int32 [256], P(('dp', 'frame')), may hold values from 1 to 77
- cotangent: bfloat16 [256, 77, 1600], P(('dp', 'frame')), may hold values from -6 to 6
- query_weight: bfloat16 [1600, 896], P('dp'), may hold values from -0.15625 to 0.15625
- key_weight: bfloat16 [1024, 896], P('dp'), may hold values from -0.1875 to 0.1875
- value_weight: bfloat16 [1024, 896], P('dp'), may hold values from -0.1875 to 0.1875
- out_weight: bfloat16 [896, 1600], P('dp'), may hold values from -0.1875 to 0.1875
Outputs:
- grad_text: bfloat16 [256, 77, 1600], P(('dp', 'frame'))
- grad_pooled: bfloat16 [256, 32, 1024], P('dp', 'frame')
Inputs may be any that keep to these rules, and one draw needn't show every extreme that they name: `lengths`: text positions at or after a clip's length are padding.
All inputs are finite; a program needn't handle non-finite values.
Results may differ from a plain program's by a relative error of at most 0.02.
The roundings to bfloat16 on the way count: a program that leaves them out, or rounds other values in their place, can miss the bound.
Values may be sent and summed in bfloat16 or wider, within the bound.
No kernel may reach another device: no remote copies, remote signals or barrier semaphores. Data moves between devices by JAX's collectives and lax.ppermute only.
A program may use at most 64 MiB of HBM per device.

v0:
```python
import functools

import jax
import jax.numpy as jnp
from jax import lax
from jax.experimental import pallas as pl
from jax.experimental.pallas import tpu as pltpu
from jax.sharding import PartitionSpec as P


HD = 64
EPSILON = 1e-05
F32 = jnp.float32
BF16 = jnp.bfloat16
LANES = 128
NT = (((1,), (1,)), ((), ()))
TN = (((0,), (0,)), ((), ()))
VMEM = pl.BlockSpec(memory_space=pltpu.VMEM)
SMEM = pl.BlockSpec(memory_space=pltpu.SMEM)


def up(value, unit):
    return -(-value // unit) * unit


def spans(total, step):
    return [(i, min(step, total - i)) for i in range(0, total, step)]


def params():
    return pltpu.CompilerParams(vmem_limit_bytes=32 * 1024 * 1024)


def cost(flops, nbytes):
    return pl.CostEstimate(flops=flops, bytes_accessed=nbytes, transcendentals=0)


def relayed(count):
    return count // 4 == 4


def pieces_of(own, count):
    def move(array, pairs):
        return lax.ppermute(array, "dp", pairs)

    def along(pairs):
        return [(4 * a + i, 4 * b + i) for a, b in pairs for i in range(4)]

    def flip(mask):
        return [(i, i ^ mask) for i in range(count)]

    pieces = {0: own}
    if relayed(count):
        place = lax.axis_index("dp") // 4
        inner = (place == 1) | (place == 2)
        swap, ends = along([(1, 2), (2, 1)]), along([(1, 0), (2, 3)])
        pieces[4] = move(own, flip(4))
        first = move(own, swap)
        second = move(pieces[4], swap)
        pieces[8] = jnp.where(inner, first, move(first, ends))
        pieces[12] = jnp.where(inner, second, move(second, ends))
    else:
        for mask in range(4, count, 4):
            pieces[mask] = move(own, flip(mask))
    for mask in range(0, count, 4):
        if mask + 2 < count:
            pieces[mask + 2] = move(pieces[mask], flip(2))
    for mask in range(0, count, 2):
        pieces[mask + 1] = move(pieces[mask], flip(1))
    return [pieces[mask] for mask in range(count)]


def sources(count):
    me = lax.axis_index("dp")
    inner = lax.rem(lax.div(lax.div(me, 4) + 1, 2), 2)
    turn = 4 * inner if relayed(count) else 0
    return [me ^ m ^ turn if m >= 8 else me ^ m for m in range(count)]


def project_kernel(count, out_rows, *refs):
    pieces = refs[:count]
    pool_ref, cot_ref, kv_ref, wkv, gs_ref, loose, wo = refs[count:]
    rows, model = cot_ref.shape
    tiles, full, _ = gs_ref.shape
    width = tiles * LANES
    depth = wkv.shape[0] // count
    _, tall, wide = loose.shape
    if full > rows:
        for j in range(tiles):
            gs_ref[j, rows:full, :] = jnp.zeros((full - rows, LANES), F32)
    for piece, source in zip(pieces, sources(count)):
        wkv[pl.ds(pl.multiple_of(source * depth, depth), depth), :] = piece[0:depth, :]
        loose[source] = piece[depth : depth + tall, 0:wide]
    for p in range(count):
        wo[p * out_rows : (p + 1) * out_rows, :] = loose[p, 0:out_rows, :]
    for at, size in spans(2 * width, 256):
        made = jnp.dot(pool_ref[...], wkv[:, at : at + size], preferred_element_type=F32)
        if at + size <= width:
            made = made.astype(BF16) * HD ** (-0.5)
        elif at < width:
            lane = at + lax.broadcasted_iota(jnp.int32, made.shape, 1)
            made = made * jnp.where(lane < width, HD ** (-0.5), 1.0)
        kv_ref[:, at : at + size] = made.astype(BF16)
    for at, size in spans(width, 256):
        made = lax.dot_general(
            cot_ref[...], wo[at : at + size, :model], NT, preferred_element_type=F32
        )
        made = made.astype(BF16).astype(F32)
        for part in range(0, size, LANES):
            gs_ref[(at + part) // LANES, 0:rows, :] = made[:, part : part + LANES]


def norm_kernel(text_ref, gain_ref, normed_ref, mean_ref, inv_ref):
    rows = text_ref.shape[0]
    step = 88 if rows % 88 == 0 else rows

    for at, size in spans(rows, step):
        x = text_ref[at : at + size, :].astype(F32)
        mean = jnp.mean(x, axis=1, keepdims=True)
        centered = x - mean
        inverse = lax.rsqrt(jnp.mean(centered * centered, axis=1, keepdims=True) + EPSILON)
        normed_ref[at : at + size, :] = (centered * inverse * gain_ref[...]).astype(BF16)
        mean_ref[at : at + size, :] = jnp.broadcast_to(mean, (size, LANES))
        inv_ref[at : at + size, :] = jnp.broadcast_to(inverse, (size, LANES))


def attend_kernel(count, clips, frames, *refs):
    pieces = refs[:count]
    lengths_ref, normed_ref, gs_ref, kv_ref, wkv, gq_ref, pool_ref, wq = refs[
        count : count + 8
    ]
    slots, qs, gkv = refs[count + 8 :]
    depth = pieces[0].shape[0]
    width = kv_ref.shape[1] // 2
    rows = normed_ref.shape[0]
    tiles, full, _ = qs.shape
    times = full // clips
    lat = kv_ref.shape[0] // (frames * clips)
    latents = lat * frames
    scale = HD ** (-0.5)
    for piece, source in zip(pieces, sources(count)):
        slots[source] = piece[...]
    if full > rows:
        for j in range(tiles):
            qs[j, rows:full, :] = jnp.zeros((full - rows, LANES), F32)
    for p in range(count):
        wq[p * depth : (p + 1) * depth, :] = slots[p]
    for at, size in spans(width, 256):
        made = jnp.dot(normed_ref[...], wq[:, at : at + size], preferred_element_type=F32)
        made = made.astype(BF16).astype(F32)
        for part in range(0, size, LANES):
            qs[(at + part) // LANES, 0:rows, :] = made[:, part : part + LANES]

    def clip(c, carry):
        length = lengths_ref[c]
        valid = lax.broadcasted_iota(jnp.int32, (times, LANES), 0) < length
        starts = [
            pl.multiple_of((f * clips + c) * lat, lat) for f in range(frames)
        ]
        for first in range(0, tiles, 2):
            group = range(first, min(first + 2, tiles))
            at = first * LANES
            wide = len(group) * LANES
            heads = wide // HD
            q = jnp.concatenate(
                [qs[j, pl.ds(c, times, stride=clips), :].astype(BF16) for j in group], 1
            )
            g = jnp.concatenate(
                [
                    jnp.where(valid, gs_ref[j, pl.ds(c, times, stride=clips), :], 0.0).astype(BF16)
                    for j in group
                ],
                1,
            )
            lane = lax.broadcasted_iota(jnp.int32, (latents, wide), 1) // HD
            k = jnp.concatenate([kv_ref[pl.ds(s, lat), at : at + wide] for s in starts], 0)
            v = jnp.concatenate(
                [kv_ref[pl.ds(s, lat), width + at : width + at + wide] for s in starts], 0
            )
            zero = jnp.zeros_like(k)
            kx = jnp.concatenate([jnp.where(lane == h, k, zero) for h in range(heads)], 0)
            vx = jnp.concatenate([jnp.where(lane == h, v, zero) for h in range(heads)], 0)
            s = lax.dot_general(kx, q, NT, preferred_element_type=F32)
            gp = lax.dot_general(vx, g, NT, preferred_element_type=F32)
            s = s.reshape(heads, latents, times)
            gp = gp.reshape(heads, latents, times)
            e = jnp.exp(s - jnp.max(s, axis=1, keepdims=True))
            probs = e * (1.0 / jnp.sum(e, axis=1, keepdims=True))
            probs_low = probs.astype(BF16)
            row = jnp.sum(probs_low.astype(F32) * gp, axis=1, keepdims=True)
            grad = (probs * (gp - row)).astype(BF16).reshape(heads * latents, times)
            probs_low = probs_low.reshape(heads * latents, times)
            gq = lax.dot_general(grad, kx, TN, preferred_element_type=F32)
            for n, j in enumerate(group):
                qs[j, pl.ds(c, times, stride=clips), :] = gq[:, n * LANES : (n + 1) * LANES]
            gk = jnp.dot(grad, q, preferred_element_type=F32)
            gv = jnp.dot(probs_low, g, preferred_element_type=F32)

            def pick(full):
                out = full[:latents]
                for h in range(1, heads):
                    out = jnp.where(lane == h, full[h * latents : (h + 1) * latents], out)
                return out

            gk = (pick(gk) * scale).astype(BF16)
            gv = pick(gv).astype(BF16)
            for f in range(frames):
                part = slice(f * lat, (f + 1) * lat)
                gkv[pl.ds(starts[f], lat), at : at + wide] = gk[part]
                gkv[pl.ds(starts[f], lat), width + at : width + at + wide] = gv[part]
        return carry

    lax.fori_loop(0, clips, clip, 0, unroll=2)
    for at, size in spans(pool_ref.shape[1], 256):
        made = lax.dot_general(
            gkv[...], wkv[at : at + size, : 2 * width], NT, preferred_element_type=F32
        )
        pool_ref[:, at : at + size] = made.astype(BF16)
    for j in range(tiles):
        gq_ref[:, j * LANES : (j + 1) * LANES] = qs[j, 0:rows, :].astype(BF16)


def text_grad_kernel(text_ref, mean_ref, inv_ref, gain_ref, gq_ref, wq_ref, out_ref, acc):
    deep = wq_ref.shape[0]
    for at, size in spans(deep, 256):
        acc[:, at : at + size] = (
            lax.dot_general(
                gq_ref[...], wq_ref[at : at + size, :], NT, preferred_element_type=F32
            )
            * gain_ref[:, at : at + size]
        )
    rows = text_ref.shape[0]
    step = 88 if rows % 88 == 0 else rows
    for at, size in spans(rows, step):
        x = text_ref[at : at + size, :].astype(F32)
        inverse = inv_ref[at : at + size, 0:1]
        unit = (x - mean_ref[at : at + size, 0:1]) * inverse
        g = acc[at : at + size, :]
        first = jnp.mean(g, axis=1, keepdims=True)
        second = jnp.mean(g * unit, axis=1, keepdims=True)
        out_ref[at : at + size, :] = (inverse * (g - first - unit * second)).astype(BF16)


def shards(
    video_tokens,
    pool_weight,
    text_states,
    norm_gain,
    lengths,
    cotangent,
    query_weight,
    key_weight,
    value_weight,
    out_weight,
    *,
    count,
    frames,
):
    visual = video_tokens.shape[3]
    lat = pool_weight.shape[1]
    clips, times, model = text_states.shape
    width = query_weight.shape[1]
    depth = query_weight.shape[0]
    kv_rows = key_weight.shape[0]
    rows = clips * times
    full = clips * up(times, 16)
    latent_rows = frames * clips * lat
    out_rows = out_weight.shape[0]
    tall = up(out_rows, 8)
    wide = up(model, LANES)
    lanes = max(2 * width, wide)
    frame = lax.axis_index("frame")

    pack = jnp.concatenate(
        [
            jnp.pad(
                jnp.concatenate([key_weight, value_weight], 1),
                ((0, 0), (0, lanes - 2 * width)),
            ),
            jnp.pad(out_weight, ((0, tall - out_rows), (0, lanes - model))),
        ],
        0,
    )
    packs = pieces_of(pack, count)
    query_pieces = pieces_of(query_weight, count)

    pooled = jnp.einsum(
        "flp,cfpv->cflv", pool_weight, video_tokens, preferred_element_type=F32
    ).astype(BF16)
    pooled = pooled.reshape(frames, clips * lat, visual)
    blocks = []
    for shift in range(frames):
        block = lax.dynamic_index_in_dim(pooled, (frame + shift) % frames, 0, keepdims=False)
        if shift:
            block = lax.ppermute(block, "frame", [(i, (i + shift) % frames) for i in range(frames)])
        blocks.append(block)
    pool_rows = jnp.concatenate(blocks, 0)

    text = jnp.transpose(text_states, (1, 0, 2)).reshape(rows, model)
    cot = jnp.transpose(cotangent, (1, 0, 2)).reshape(rows, model)
    gain = norm_gain.reshape(1, model)

    normed, mean, inverse = pl.pallas_call(
        norm_kernel,
        name="norm",
        out_shape=(
            jax.ShapeDtypeStruct((rows, model), BF16),
            jax.ShapeDtypeStruct((rows, LANES), F32),
            jax.ShapeDtypeStruct((rows, LANES), F32),
        ),
        in_specs=[VMEM, VMEM],
        out_specs=(VMEM, VMEM, VMEM),
        compiler_params=params(),
        cost_estimate=cost(rows * model * 10, rows * model * 4),
    )(text, gain)

    keys_values, kv_full, grad_att = pl.pallas_call(
        functools.partial(project_kernel, count, out_rows),
        name="project",
        out_shape=(
            jax.ShapeDtypeStruct((latent_rows, 2 * width), BF16),
            jax.ShapeDtypeStruct((count * kv_rows, lanes), BF16),
            jax.ShapeDtypeStruct((width // LANES, full, LANES), F32),
        ),
        in_specs=[VMEM] * (count + 2),
        out_specs=(VMEM, VMEM, VMEM),
        scratch_shapes=[
            pltpu.VMEM((count, tall, wide), BF16),
            pltpu.VMEM((width, wide), BF16),
        ],
        compiler_params=params(),
        cost_estimate=cost(
            2 * rows * model * width + 4 * latent_rows * visual * width,
            4 * model * width + 4 * visual * width,
        ),
    )(*packs, pool_rows, cot)

    grad_queries, pool_grad, query_full = pl.pallas_call(
        functools.partial(attend_kernel, count, clips, frames),
        name="attend",
        out_shape=(
            jax.ShapeDtypeStruct((rows, width), BF16),
            jax.ShapeDtypeStruct((latent_rows, visual), BF16),
            jax.ShapeDtypeStruct((model, width), BF16),
        ),
        in_specs=[VMEM] * count + [SMEM, VMEM, VMEM, VMEM, VMEM],
        out_specs=(VMEM, VMEM, VMEM),
        scratch_shapes=[
            pltpu.VMEM((count, depth, width), BF16),
            pltpu.VMEM((width // LANES, full, LANES), F32),
            pltpu.VMEM((latent_rows, 2 * width), BF16),
        ],
        compiler_params=params(),
        cost_estimate=cost(4 * rows * model * width, 8 * model * width),
    )(*query_pieces, lengths, normed, grad_att, keys_values, kv_full)

    pool_grad = pool_grad.reshape(frames, clips, lat, visual)
    grad_pooled = jnp.zeros((frames, clips, lat, visual), BF16)
    for shift in range(frames):
        block = pool_grad[shift]
        if shift:
            block = lax.ppermute(
                block, "frame", [(i, (i - shift) % frames) for i in range(frames)]
            )
        grad_pooled = lax.dynamic_update_index_in_dim(
            grad_pooled, block, (frame + shift) % frames, 0
        )
    grad_pooled = grad_pooled.reshape(frames * clips, lat, visual)

    grad_text = pl.pallas_call(
        text_grad_kernel,
        name="text_grad",
        out_shape=jax.ShapeDtypeStruct((rows, model), BF16),
        in_specs=[VMEM] * 6,
        out_specs=VMEM,
        scratch_shapes=[pltpu.VMEM((rows, model), F32)],
        compiler_params=params(),
        cost_estimate=cost(2 * rows * model * width, 2 * model * width + 4 * rows * model),
    )(text, mean, inverse, gain, grad_queries, query_full)
    grad_text = jnp.transpose(grad_text.reshape(times, clips, model), (1, 0, 2))
    return (grad_text, grad_pooled)


def solution(mesh):
    in_specs = (
        P("dp", "frame", None, None),
        P("frame", None, None),
        P(("dp", "frame"), None, None),
        P(),
        P(("dp", "frame")),
        P(("dp", "frame"), None, None),
        P("dp", None),
        P("dp", None),
        P("dp", None),
        P("dp", None),
    )
    out_specs = (P(("dp", "frame"), None, None), P("dp", "frame", None))
    count = mesh.shape["dp"]
    body = functools.partial(shards, count=count, frames=mesh.shape["frame"])

    return jax.shard_map(body, mesh=mesh, in_specs=in_specs, out_specs=out_specs, check_vma=False)
```

profile of v0, /device:TPU:0, one launch (start us, length us, event | category | flops | bytes accessed | tf_op | source)
XLA Modules:
  0.0 124.8 jit_solution(979202855165486931)
XLA Ops:
  0.6 0.0 copy-start
  0.6 0.0 copy-start.3
  0.7 3.1 %collective-permute-start.3 = (bf16[100,896]{1,0:T(8,128)(2,1)}, bf16[100,896]{1,0:T(8,128)(2,1)S(1)}, u32[]{:S(2)}, u32[]{:S(2)}) collective-permute-start(bf16[100,896]{1,0:T(8,128)(2,1)} %refs_0_.1), channel_id=1, source_target_pairs={{0,8},{2,10},{4,12},{6,14},{8,0},{10,2},{12,4},{14,6},{16,24},{18,... | collective-permute-start | bytes 537608 | tf_op jit(solution)/shard_map/ppermute | solution.py:44
  3.8 1.3 %collective-permute-start.7 = (bf16[100,896]{1,0:T(8,128)(2,1)}, bf16[100,896]{1,0:T(8,128)(2,1)}, u32[]{:S(2)}, u32[]{:S(2)}) collective-permute-start(bf16[100,896]{1,0:T(8,128)(2,1)} %refs_0_.1), channel_id=1, source_target_pairs={{8,16},{10,18},{12,20},{14,22},{16,8},{18,10},{20,12},{22,14},{9,1... | collective-permute-start | bytes 537608 | tf_op jit(solution)/shard_map/ppermute | solution.py:44
  5.1 1.1 fusion.2.refs_0_
  6.2 3.8 %collective-permute-start.20 = (bf16[120,1792]{1,0:T(8,128)(2,1)S(1)}, bf16[120,1792]{1,0:T(8,128)(2,1)S(1)}, u32[]{:S(2)}, u32[]{:S(2)}) collective-permute-start(bf16[120,1792]{1,0:T(8,128)(2,1)S(1)} %fusion.2.refs_0_), channel_id=1, source_target_pairs={{0,8},{2,10},{4,12},{6,14},{8,0},{10,2},{12,4},{14,6},{16,24},{18,... | collective-permute-start | bytes 1290248 | tf_op jit(solution)/shard_map/ppermute | solution.py:44
  10.0 0.7 collective-permute-start.24
  10.7 1.6 %collective-permute-start.1 = (bf16[100,896]{1,0:T(8,128)(2,1)}, bf16[100,896]{1,0:T(8,128)(2,1)S(1)}, u32[]{:S(2)}, u32[]{:S(2)}) collective-permute-start(bf16[100,896]{1,0:T(8,128)(2,1)} %refs_0_.1), channel_id=1, source_target_pairs={{0,4},{2,6},{4,0},{6,2},{8,12},{10,14},{12,8},{14,10},{16,20},{18,... | collective-permute-start | bytes 537608 | tf_op jit(solution)/shard_map/ppermute | solution.py:44
  12.2 0.0 collective-permute-done.3.refs_4_
  12.2 1.3 %collective-permute-start.12 = (bf16[100,896]{1,0:T(8,128)(2,1)S(1)}, bf16[100,896]{1,0:T(8,128)(2,1)}, u32[]{:S(2)}, u32[]{:S(2)}) collective-permute-start(bf16[100,896]{1,0:T(8,128)(2,1)S(1)} %collective-permute-done.3.refs_4_), channel_id=1, source_target_pairs={{8,16},{10,18},{12,20},{14,22},{16,8},{18,10},{20,12},{22,14},{9,1... | collective-permute-start | bytes 537608 | tf_op jit(solution)/shard_map/ppermute | solution.py:44
  13.6 0.0 collective-permute-done.7
  13.6 1.3 %collective-permute-start.8 = (bf16[100,896]{1,0:T(8,128)(2,1)}, bf16[100,896]{1,0:T(8,128)(2,1)}, u32[]{:S(2)}, u32[]{:S(2)}) collective-permute-start(bf16[100,896]{1,0:T(8,128)(2,1)} %collective-permute-done.7), channel_id=1, source_target_pairs={{8,0},{10,2},{12,4},{14,6},{16,24},{18,26},{20,28},{22,30},{9,1},{... | collective-permute-start | bytes 537608 | tf_op jit(solution)/shard_map/ppermute | solution.py:44
  14.9 1.0 convolution_convert_fusion
  15.9 0.0 copy-start.8
  15.9 0.0 copy-start.1
  15.9 0.0 collective-permute-done.12
  16.0 0.1 collective-permute-start
  16.0 7.4 %collective-permute-done.8 = bf16[100,896]{1,0:T(8,128)(2,1)} collective-permute-done((bf16[100,896]{1,0:T(8,128)(2,1)}, bf16[100,896]{1,0:T(8,128)(2,1)}, u32[]{:S(2)}, u32[]{:S(2)}) %collective-permute-start.8) | collective-permute-done | bytes 179232 | tf_op jit(solution)/shard_map/ppermute | solution.py:44
  23.4 1.3 %collective-permute-start.13 = (bf16[100,896]{1,0:T(8,128)(2,1)}, bf16[100,896]{1,0:T(8,128)(2,1)S(1)}, u32[]{:S(2)}, u32[]{:S(2)}) collective-permute-start(bf16[100,896]{1,0:T(8,128)(2,1)} %collective-permute-done.12), channel_id=1, source_target_pairs={{8,0},{10,2},{12,4},{14,6},{16,24},{18,26},{20,28},{22,30},{9,1},{... | collective-permute-start | bytes 537608 | tf_op jit(solution)/shard_map/ppermute | solution.py:44
  24.7 0.7 collective-permute-start.29
  25.4 0.0 collective-permute-done.24
  25.4 1.3 %collective-permute-start.25 = (bf16[120,1792]{1,0:T(8,128)(2,1)S(1)}, bf16[120,1792]{1,0:T(8,128)(2,1)S(1)}, u32[]{:S(2)}, u32[]{:S(2)}) collective-permute-start(bf16[120,1792]{1,0:T(8,128)(2,1)S(1)} %collective-permute-done.24), channel_id=1, source_target_pairs={{8,0},{10,2},{12,4},{14,6},{16,24},{18,26},{20,28},{22,30},{9,1},{... | collective-permute-start | bytes 1290248 | tf_op jit(solution)/shard_map/ppermute | solution.py:44
  26.7 1.0 broadcast_select_fusion.3.refs_8_
  27.7 6.2 %collective-permute-done.13 = bf16[100,896]{1,0:T(8,128)(2,1)S(1)} collective-permute-done((bf16[100,896]{1,0:T(8,128)(2,1)}, bf16[100,896]{1,0:T(8,128)(2,1)S(1)}, u32[]{:S(2)}, u32[]{:S(2)}) %collective-permute-start.13) | collective-permute-done | bytes 179232 | tf_op jit(solution)/shard_map/ppermute | solution.py:44
  33.9 1.5 %collective-permute-start.34 = (bf16[128,1024]{1,0:T(8,128)(2,1)S(1)}, bf16[128,1024]{1,0:T(8,128)(2,1)S(1)}, u32[]{:S(2)}, u32[]{:S(2)}) collective-permute-start(bf16[128,1024]{1,0:T(8,128)(2,1)S(1)} %get-tuple-element.23), channel_id=1, source_target_pairs={{0,1},{1,0},{2,3},{3,2},{4,5},{5,4},{6,7},{7,6},{8,9},{9,8},{10,11... | collective-permute-start | bytes 786440 | tf_op jit(solution)/shard_map/ppermute | solution.py:295
  35.5 0.0 collective-permute-done.1.refs_2_
  35.5 1.6 %collective-permute-start.5 = (bf16[100,896]{1,0:T(8,128)(2,1)S(1)}, bf16[100,896]{1,0:T(8,128)(2,1)S(1)}, u32[]{:S(2)}, u32[]{:S(2)}) collective-permute-start(bf16[100,896]{1,0:T(8,128)(2,1)S(1)} %collective-permute-done.3.refs_4_), channel_id=1, source_target_pairs={{0,4},{2,6},{4,0},{6,2},{8,12},{10,14},{12,8},{14,10},{16,20},{18,... | collective-permute-start | bytes 537608 | tf_op jit(solution)/shard_map/ppermute | solution.py:44
  37.0 6.3 %collective-permute-done.25 = bf16[120,1792]{1,0:T(8,128)(2,1)S(1)} collective-permute-done((bf16[120,1792]{1,0:T(8,128)(2,1)S(1)}, bf16[120,1792]{1,0:T(8,128)(2,1)S(1)}, u32[]{:S(2)}, u32[]{:S(2)}) %collective-permute-start.25) | collective-permute-done | bytes 430112 | tf_op jit(solution)/shard_map/ppermute | solution.py:44
  43.3 1.3 %collective-permute-start.30 = (bf16[120,1792]{1,0:T(8,128)(2,1)S(1)}, bf16[120,1792]{1,0:T(8,128)(2,1)S(1)}, u32[]{:S(2)}, u32[]{:S(2)}) collective-permute-start(bf16[120,1792]{1,0:T(8,128)(2,1)S(1)} %collective-permute-done.29), channel_id=1, source_target_pairs={{8,0},{10,2},{12,4},{14,6},{16,24},{18,26},{20,28},{22,30},{9,1},{... | collective-permute-start | bytes 1290248 | tf_op jit(solution)/shard_map/ppermute | solution.py:44
  44.6 0.1 broadcast_select_fusion.1.refs_8_
  44.6 0.0 copy-start.2
  44.7 1.6 %collective-permute-start.18 = (bf16[120,1792]{1,0:T(8,128)(2,1)S(1)}, bf16[120,1792]{1,0:T(8,128)(2,1)S(1)}, u32[]{:S(2)}, u32[]{:S(2)}) collective-permute-start(bf16[120,1792]{1,0:T(8,128)(2,1)S(1)} %fusion.2.refs_0_), channel_id=1, source_target_pairs={{0,4},{2,6},{4,0},{6,2},{8,12},{10,14},{12,8},{14,10},{16,20},{18,... | collective-permute-start | bytes 1290248 | tf_op jit(solution)/shard_map/ppermute | solution.py:44
  46.2 0.5 collective-permute-start.2
  46.7 0.5 collective-permute-start.10
  47.3 9.3 %collective-permute-done.30 = bf16[120,1792]{1,0:T(8,128)(2,1)S(1)} collective-permute-done((bf16[120,1792]{1,0:T(8,128)(2,1)S(1)}, bf16[120,1792]{1,0:T(8,128)(2,1)S(1)}, u32[]{:S(2)}, u32[]{:S(2)}) %collective-permute-start.30) | collective-permute-done | bytes 430112 | tf_op jit(solution)/shard_map/ppermute | solution.py:44
  56.6 1.5 %collective-permute-start.15 = (bf16[100,896]{1,0:T(8,128)(2,1)S(1)}, bf16[100,896]{1,0:T(8,128)(2,1)S(1)}, u32[]{:S(2)}, u32[]{:S(2)}) collective-permute-start(bf16[100,896]{1,0:T(8,128)(2,1)S(1)} %broadcast_select_fusion.2.refs_12_), channel_id=1, source_target_pairs={{0,4},{2,6},{4,0},{6,2},{8,12},{10,14},{12,8},{14,10},{16,20},{18,... | collective-permute-start | bytes 537608 | tf_op jit(solution)/shard_map/ppermute | solution.py:44
  58.1 0.1 broadcast_select_fusion.refs_12_
  58.2 0.6 collective-permute-start.22
  58.8 0.5 collective-permute-start.19
  59.3 2.2 %collective-permute-done.10.refs_10_ = bf16[100,896]{1,0:T(8,128)(2,1)S(1)} collective-permute-done((bf16[100,896]{1,0:T(8,128)(2,1)S(1)}, bf16[100,896]{1,0:T(8,128)(2,1)S(1)}, u32[]{:S(2)}, u32[]{:S(2)}) %collective-permute-start.10) | collective-permute-done | bytes 179232 | tf_op jit(solution)/shard_map/ppermute | solution.py:44
  61.5 1.5 %collective-permute-start.27 = (bf16[120,1792]{1,0:T(8,128)(2,1)S(1)}, bf16[120,1792]{1,0:T(8,128)(2,1)S(1)}, u32[]{:S(2)}, u32[]{:S(2)}) collective-permute-start(bf16[120,1792]{1,0:T(8,128)(2,1)S(1)} %broadcast_select_fusion.1.refs_8_), channel_id=1, source_target_pairs={{0,4},{2,6},{4,0},{6,2},{8,12},{10,14},{12,8},{14,10},{16,20},{18,... | collective-permute-start | bytes 1290248 | tf_op jit(solution)/shard_map/ppermute | solution.py:44
  63.0 2.5 %collective-permute-done.15.refs_14_ = bf16[100,896]{1,0:T(8,128)(2,1)S(1)} collective-permute-done((bf16[100,896]{1,0:T(8,128)(2,1)S(1)}, bf16[100,896]{1,0:T(8,128)(2,1)S(1)}, u32[]{:S(2)}, u32[]{:S(2)}) %collective-permute-start.15) | collective-permute-done | bytes 179232 | tf_op jit(solution)/shard_map/ppermute | solution.py:44
  65.5 1.5 %collective-permute-start.32 = (bf16[120,1792]{1,0:T(8,128)(2,1)S(1)}, bf16[120,1792]{1,0:T(8,128)(2,1)S(1)}, u32[]{:S(2)}, u32[]{:S(2)}) collective-permute-start(bf16[120,1792]{1,0:T(8,128)(2,1)S(1)} %broadcast_select_fusion.refs_12_), channel_id=1, source_target_pairs={{0,4},{2,6},{4,0},{6,2},{8,12},{10,14},{12,8},{14,10},{16,20},{18,... | collective-permute-start | bytes 1290248 | tf_op jit(solution)/shard_map/ppermute | solution.py:44
  67.0 7.7 %collective-permute-done.22.refs_6_ = bf16[120,1792]{1,0:T(8,128)(2,1)S(1)} collective-permute-done((bf16[120,1792]{1,0:T(8,128)(2,1)S(1)}, bf16[120,1792]{1,0:T(8,128)(2,1)S(1)}, u32[]{:S(2)}, u32[]{:S(2)}) %collective-permute-start.22) | collective-permute-done | bytes 430112 | tf_op jit(solution)/shard_map/ppermute | solution.py:44
  74.7 0.5 collective-permute-start.23
  75.2 0.1 collective-permute-start.31
  75.3 8.6 %collective-permute-done.27.refs_10_ = bf16[120,1792]{1,0:T(8,128)(2,1)S(1)} collective-permute-done((bf16[120,1792]{1,0:T(8,128)(2,1)S(1)}, bf16[120,1792]{1,0:T(8,128)(2,1)S(1)}, u32[]{:S(2)}, u32[]{:S(2)}) %collective-permute-start.27) | collective-permute-done | bytes 430112 | tf_op jit(solution)/shard_map/ppermute | solution.py:44
  83.9 7.9 %collective-permute-done.32.refs_14_ = bf16[120,1792]{1,0:T(8,128)(2,1)S(1)} collective-permute-done((bf16[120,1792]{1,0:T(8,128)(2,1)S(1)}, bf16[120,1792]{1,0:T(8,128)(2,1)S(1)}, u32[]{:S(2)}, u32[]{:S(2)}) %collective-permute-start.32) | collective-permute-done | bytes 430112 | tf_op jit(solution)/shard_map/ppermute | solution.py:44
  91.8 1.3 %norm.1 = (bf16[616,1600]{1,0:T(8,128)(2,1)S(1)}, f32[616,128]{1,0:T(8,128)S(1)}, f32[616,128]{1,0:T(8,128)S(1)}) custom-call(bf16[616,1600]{1,0:T(8,128)(2,1)S(1)} %bitcast.30, f32[1,1600]{1,0:T(1,128)S(1)} %reshape.35.gain_ref), custom_call_target="tpu_custom_call" | custom-call | flops 9856000 | bytes 3942400 | tf_op jit(solution)/shard_map/norm/pallas_call | solution.py:303
  93.2 0.6 collective-permute-start.9
  93.7 0.1 collective-permute-start.6
  93.8 0.4 collective-permute-start.14
  94.3 0.1 collective-permute-start.11
  94.3 0.4 collective-permute-start.16
  94.8 3.9 %project.1 = (bf16[256,1792]{1,0:T(8,128)(2,1)S(1)}, bf16[1024,1792]{1,0:T(8,128)(2,1)S(1)}, f32[7,640,128]{2,1,0:T(8,128)S(1)}) custom-call(bf16[120,1792]{1,0:T(8,128)(2,1)S(1)} %fusion.2.refs_0_, bf16[120,1792]{1,0:T(8,128)(2,1)S(1)} %collective-permute-done.17.refs_1_, bf16[120,1792]{1,0:T(8,128)(2,1)S(1)} %collective-permute-done.18.refs_2_, ...), custom_call_target="tpu_custom_call" | custom-call | flops 2705719296 | bytes 9404416 | tf_op jit(solution)/shard_map/project/pallas_call | solution.py:317
  98.7 1.4 %copy-done.5 = f32[7,640,128]{2,1,0:T(8,128)} copy-done((f32[7,640,128]{2,1,0:T(8,128)}, f32[7,640,128]{2,1,0:T(8,128)S(1)}, u32[]{:S(2)}) %copy-start.5) | copy-done | bytes 2293784
  100.2 1.6 %copy-done.6 = f32[7,640,128]{2,1,0:T(8,128)S(1)} copy-done((f32[7,640,128]{2,1,0:T(8,128)S(1)}, f32[7,640,128]{2,1,0:T(8,128)}, u32[]{:S(2)}) %copy-start.6) | copy-done | bytes 2293784
  101.8 13.7 %attend.1 = (bf16[616,896]{1,0:T(8,128)(2,1)S(1)}, bf16[256,1024]{1,0:T(8,128)(2,1)S(1)}, bf16[1600,896]{1,0:T(8,128)(2,1)S(1)}) custom-call(bf16[100,896]{1,0:T(8,128)(2,1)S(1)} %copy-done.3, bf16[100,896]{1,0:T(8,128)(2,1)S(1)} %collective-permute-done.refs_1_, bf16[100,896]{1,0:T(8,128)(2,1)S(1)} %collective-permute-done.1.refs_2_, ...), custom_call_target="tpu_custom_call" | custom-call | flops 3532390400 | bytes 11468800 | tf_op jit(solution)/shard_map/attend/pallas_call | solution.py:338
  115.6 1.6 %collective-permute-start.35 = (bf16[8,16,1024]{2,1,0:T(8,128)(2,1)S(1)}, bf16[8,16,1024]{2,1,0:T(8,128)(2,1)S(1)}, u32[]{:S(2)}, u32[]{:S(2)}) collective-permute-start(bf16[8,16,1024]{2,1,0:T(8,128)(2,1)S(1)} %bitcast.37), channel_id=1, source_target_pairs={{0,1},{1,0},{2,3},{3,2},{4,5},{5,4},{6,7},{7,6},{8,9},{9,8},{10,11... | collective-permute-start | bytes 786440 | tf_op jit(solution)/shard_map/ppermute | solution.py:362
  117.2 0.1 broadcast_in_dim.8
  117.2 4.8 %text_grad.1 = bf16[616,1600]{1,0:T(8,128)(2,1)} custom-call(bf16[616,1600]{1,0:T(8,128)(2,1)S(1)} %bitcast.31, f32[616,128]{1,0:T(8,128)S(1)} %get-tuple-element.11.mean_ref, f32[616,128]{1,0:T(8,128)S(1)} %get-tuple-element.12.inv_ref, f32[1,1600]{1,0:T(1,128)S(1)} %reshape.35.gain_ref, bf16[616,896]{1,0:T(8,128)(2,1)S(1)} %get-tuple-element.17.gq_ref, ...), custom_call_target="tpu_custom_call" | custom-call | flops 1766195200 | bytes 6809600 | tf_op jit(solution)/shard_map/text_grad/pallas_call | solution.py:370
  122.0 1.9 %collective-permute-done.35 = bf16[8,16,1024]{2,1,0:T(8,128)(2,1)S(1)} collective-permute-done((bf16[8,16,1024]{2,1,0:T(8,128)(2,1)S(1)}, bf16[8,16,1024]{2,1,0:T(8,128)(2,1)S(1)}, u32[]{:S(2)}, u32[]{:S(2)}) %collective-permute-start.35) | collective-permute-done | bytes 262176 | tf_op jit(solution)/shard_map/ppermute | solution.py:362
  124.0 0.0 copy-start.7
  124.0 0.8 copy-done.7
  (43 shorter events, 0.3 us)
Async XLA Ops:
  0.6 14.2 %copy-start = (bf16[16,1,32,1024]{3,2,1,0:T(8,128)(2,1)S(1)}, bf16[16,1,32,1024]{3,2,1,0:T(8,128)(2,1)}, u32[]{:S(2)}) copy-start(bf16[16,1,32,1024]{3,2,1,0:T(8,128)(2,1)} %param.10) | copy-start | bytes 3145732
  0.6 15.3 %copy-start.3 = (bf16[100,896]{1,0:T(8,128)(2,1)S(1)}, bf16[100,896]{1,0:T(8,128)(2,1)}, u32[]{:S(2)}) copy-start(bf16[100,896]{1,0:T(8,128)(2,1)} %refs_0_.1) | copy-start | bytes 537604
  0.7 11.6 %collective-permute-start.3 = (bf16[100,896]{1,0:T(8,128)(2,1)}, bf16[100,896]{1,0:T(8,128)(2,1)S(1)}, u32[]{:S(2)}, u32[]{:S(2)}) collective-permute-start(bf16[100,896]{1,0:T(8,128)(2,1)} %refs_0_.1), channel_id=1, source_target_pairs={{0,8},{2,10},{4,12},{6,14},{8,0},{10,2},{12,4},{14,6},{16,24},{18,... | collective-permute-start | bytes 537608 | tf_op jit(solution)/shard_map/ppermute | solution.py:44
  3.8 9.8 %collective-permute-start.7 = (bf16[100,896]{1,0:T(8,128)(2,1)}, bf16[100,896]{1,0:T(8,128)(2,1)}, u32[]{:S(2)}, u32[]{:S(2)}) collective-permute-start(bf16[100,896]{1,0:T(8,128)(2,1)} %refs_0_.1), channel_id=1, source_target_pairs={{8,16},{10,18},{12,20},{14,22},{16,8},{18,10},{20,12},{22,14},{9,1... | collective-permute-start | bytes 537608 | tf_op jit(solution)/shard_map/ppermute | solution.py:44
  6.2 18.5 %collective-permute-start.20 = (bf16[120,1792]{1,0:T(8,128)(2,1)S(1)}, bf16[120,1792]{1,0:T(8,128)(2,1)S(1)}, u32[]{:S(2)}, u32[]{:S(2)}) collective-permute-start(bf16[120,1792]{1,0:T(8,128)(2,1)S(1)} %fusion.2.refs_0_), channel_id=1, source_target_pairs={{0,8},{2,10},{4,12},{6,14},{8,0},{10,2},{12,4},{14,6},{16,24},{18,... | collective-permute-start | bytes 1290248 | tf_op jit(solution)/shard_map/ppermute | solution.py:44
  10.0 15.4 %collective-permute-start.24 = (bf16[120,1792]{1,0:T(8,128)(2,1)S(1)}, bf16[120,1792]{1,0:T(8,128)(2,1)S(1)}, u32[]{:S(2)}, u32[]{:S(2)}) collective-permute-start(bf16[120,1792]{1,0:T(8,128)(2,1)S(1)} %fusion.2.refs_0_), channel_id=1, source_target_pairs={{8,16},{10,18},{12,20},{14,22},{16,8},{18,10},{20,12},{22,14},{9,1... | collective-permute-start | bytes 1290248 | tf_op jit(solution)/shard_map/ppermute | solution.py:44
  10.7 24.8 %collective-permute-start.1 = (bf16[100,896]{1,0:T(8,128)(2,1)}, bf16[100,896]{1,0:T(8,128)(2,1)S(1)}, u32[]{:S(2)}, u32[]{:S(2)}) collective-permute-start(bf16[100,896]{1,0:T(8,128)(2,1)} %refs_0_.1), channel_id=1, source_target_pairs={{0,4},{2,6},{4,0},{6,2},{8,12},{10,14},{12,8},{14,10},{16,20},{18,... | collective-permute-start | bytes 537608 | tf_op jit(solution)/shard_map/ppermute | solution.py:44
  12.2 3.7 %collective-permute-start.12 = (bf16[100,896]{1,0:T(8,128)(2,1)S(1)}, bf16[100,896]{1,0:T(8,128)(2,1)}, u32[]{:S(2)}, u32[]{:S(2)}) collective-permute-start(bf16[100,896]{1,0:T(8,128)(2,1)S(1)} %collective-permute-done.3.refs_4_), channel_id=1, source_target_pairs={{8,16},{10,18},{12,20},{14,22},{16,8},{18,10},{20,12},{22,14},{9,1... | collective-permute-start | bytes 537608 | tf_op jit(solution)/shard_map/ppermute | solution.py:44
  13.6 9.9 %collective-permute-start.8 = (bf16[100,896]{1,0:T(8,128)(2,1)}, bf16[100,896]{1,0:T(8,128)(2,1)}, u32[]{:S(2)}, u32[]{:S(2)}) collective-permute-start(bf16[100,896]{1,0:T(8,128)(2,1)} %collective-permute-done.7), channel_id=1, source_target_pairs={{8,0},{10,2},{12,4},{14,6},{16,24},{18,26},{20,28},{22,30},{9,1},{... | collective-permute-start | bytes 537608 | tf_op jit(solution)/shard_map/ppermute | solution.py:44
  15.9 75.9 %copy-start.8 = (f32[1600]{0:T(1024)S(1)}, f32[1600]{0:T(1024)}, u32[]{:S(2)}) copy-start(f32[1600]{0:T(1024)} %param.13) | copy-start | bytes 19204
  15.9 75.9 %copy-start.1 = (bf16[8,77,1600]{2,0,1:T(8,128)(2,1)S(1)}, bf16[8,77,1600]{2,0,1:T(8,128)(2,1)}, u32[]{:S(2)}) copy-start(bf16[8,77,1600]{2,0,1:T(8,128)(2,1)} %param.12) | copy-start | bytes 5913604
  16.0 28.7 %collective-permute-start = (bf16[100,896]{1,0:T(8,128)(2,1)S(1)}, bf16[100,896]{1,0:T(8,128)(2,1)S(1)}, u32[]{:S(2)}, u32[]{:S(2)}) collective-permute-start(bf16[100,896]{1,0:T(8,128)(2,1)S(1)} %copy-done.3), channel_id=1, source_target_pairs={{0,2},{2,0},{4,6},{6,4},{8,10},{10,8},{12,14},{14,12},{16,18},{18,... | collective-permute-start | bytes 537608 | tf_op jit(solution)/shard_map/ppermute | solution.py:44
  23.4 10.5 %collective-permute-start.13 = (bf16[100,896]{1,0:T(8,128)(2,1)}, bf16[100,896]{1,0:T(8,128)(2,1)S(1)}, u32[]{:S(2)}, u32[]{:S(2)}) collective-permute-start(bf16[100,896]{1,0:T(8,128)(2,1)} %collective-permute-done.12), channel_id=1, source_target_pairs={{8,0},{10,2},{12,4},{14,6},{16,24},{18,26},{20,28},{22,30},{9,1},{... | collective-permute-start | bytes 537608 | tf_op jit(solution)/shard_map/ppermute | solution.py:44
  24.7 12.3 %collective-permute-start.29 = (bf16[120,1792]{1,0:T(8,128)(2,1)S(1)}, bf16[120,1792]{1,0:T(8,128)(2,1)S(1)}, u32[]{:S(2)}, u32[]{:S(2)}) collective-permute-start(bf16[120,1792]{1,0:T(8,128)(2,1)S(1)} %collective-permute-done.20.refs_4_), channel_id=1, source_target_pairs={{8,16},{10,18},{12,20},{14,22},{16,8},{18,10},{20,12},{22,14},{9,1... | collective-permute-start | bytes 1290248 | tf_op jit(solution)/shard_map/ppermute | solution.py:44
  25.4 17.9 %collective-permute-start.25 = (bf16[120,1792]{1,0:T(8,128)(2,1)S(1)}, bf16[120,1792]{1,0:T(8,128)(2,1)S(1)}, u32[]{:S(2)}, u32[]{:S(2)}) collective-permute-start(bf16[120,1792]{1,0:T(8,128)(2,1)S(1)} %collective-permute-done.24), channel_id=1, source_target_pairs={{8,0},{10,2},{12,4},{14,6},{16,24},{18,26},{20,28},{22,30},{9,1},{... | collective-permute-start | bytes 1290248 | tf_op jit(solution)/shard_map/ppermute | solution.py:44
  33.9 12.3 %collective-permute-start.34 = (bf16[128,1024]{1,0:T(8,128)(2,1)S(1)}, bf16[128,1024]{1,0:T(8,128)(2,1)S(1)}, u32[]{:S(2)}, u32[]{:S(2)}) collective-permute-start(bf16[128,1024]{1,0:T(8,128)(2,1)S(1)} %get-tuple-element.23), channel_id=1, source_target_pairs={{0,1},{1,0},{2,3},{3,2},{4,5},{5,4},{6,7},{7,6},{8,9},{9,8},{10,11... | collective-permute-start | bytes 786440 | tf_op jit(solution)/shard_map/ppermute | solution.py:295
  35.5 10.8 %collective-permute-start.5 = (bf16[100,896]{1,0:T(8,128)(2,1)S(1)}, bf16[100,896]{1,0:T(8,128)(2,1)S(1)}, u32[]{:S(2)}, u32[]{:S(2)}) collective-permute-start(bf16[100,896]{1,0:T(8,128)(2,1)S(1)} %collective-permute-done.3.refs_4_), channel_id=1, source_target_pairs={{0,4},{2,6},{4,0},{6,2},{8,12},{10,14},{12,8},{14,10},{16,20},{18,... | collective-permute-start | bytes 537608 | tf_op jit(solution)/shard_map/ppermute | solution.py:44
  37.0 9.7 %collective-permute-start.4 = (bf16[100,896]{1,0:T(8,128)(2,1)S(1)}, bf16[100,896]{1,0:T(8,128)(2,1)S(1)}, u32[]{:S(2)}, u32[]{:S(2)}) collective-permute-start(bf16[100,896]{1,0:T(8,128)(2,1)S(1)} %collective-permute-done.3.refs_4_), channel_id=1, source_target_pairs={{0,2},{2,0},{4,6},{6,4},{8,10},{10,8},{12,14},{14,12},{16,18},{18,... | collective-permute-start | bytes 537608 | tf_op jit(solution)/shard_map/ppermute | solution.py:44
  43.3 13.3 %collective-permute-start.30 = (bf16[120,1792]{1,0:T(8,128)(2,1)S(1)}, bf16[120,1792]{1,0:T(8,128)(2,1)S(1)}, u32[]{:S(2)}, u32[]{:S(2)}) collective-permute-start(bf16[120,1792]{1,0:T(8,128)(2,1)S(1)} %collective-permute-done.29), channel_id=1, source_target_pairs={{8,0},{10,2},{12,4},{14,6},{16,24},{18,26},{20,28},{22,30},{9,1},{... | collective-permute-start | bytes 1290248 | tf_op jit(solution)/shard_map/ppermute | solution.py:44
  44.6 50.1 %copy-start.2 = (bf16[8,77,1600]{2,0,1:T(8,128)(2,1)S(1)}, bf16[8,77,1600]{2,0,1:T(8,128)(2,1)}, u32[]{:S(2)}) copy-start(bf16[8,77,1600]{2,0,1:T(8,128)(2,1)} %param.15) | copy-start | bytes 5913604
  44.7 14.1 %collective-permute-start.18 = (bf16[120,1792]{1,0:T(8,128)(2,1)S(1)}, bf16[120,1792]{1,0:T(8,128)(2,1)S(1)}, u32[]{:S(2)}, u32[]{:S(2)}) collective-permute-start(bf16[120,1792]{1,0:T(8,128)(2,1)S(1)} %fusion.2.refs_0_), channel_id=1, source_target_pairs={{0,4},{2,6},{4,0},{6,2},{8,12},{10,14},{12,8},{14,10},{16,20},{18,... | collective-permute-start | bytes 1290248 | tf_op jit(solution)/shard_map/ppermute | solution.py:44
  46.2 12.6 %collective-permute-start.17 = (bf16[120,1792]{1,0:T(8,128)(2,1)S(1)}, bf16[120,1792]{1,0:T(8,128)(2,1)S(1)}, u32[]{:S(2)}, u32[]{:S(2)}) collective-permute-start(bf16[120,1792]{1,0:T(8,128)(2,1)S(1)} %fusion.2.refs_0_), channel_id=1, source_target_pairs={{0,2},{2,0},{4,6},{6,4},{8,10},{10,8},{12,14},{14,12},{16,18},{18,... | collective-permute-start | bytes 1290248 | tf_op jit(solution)/shard_map/ppermute | solution.py:44
  46.2 11.9 %collective-permute-start.2 = (bf16[100,896]{1,0:T(8,128)(2,1)S(1)}, bf16[100,896]{1,0:T(8,128)(2,1)S(1)}, u32[]{:S(2)}, u32[]{:S(2)}) collective-permute-start(bf16[100,896]{1,0:T(8,128)(2,1)S(1)} %collective-permute-done.1.refs_2_), channel_id=1, source_target_pairs={{0,2},{2,0},{4,6},{6,4},{8,10},{10,8},{12,14},{14,12},{16,18},{18,... | collective-permute-start | bytes 537608 | tf_op jit(solution)/shard_map/ppermute | solution.py:44
  46.7 14.8 %collective-permute-start.10 = (bf16[100,896]{1,0:T(8,128)(2,1)S(1)}, bf16[100,896]{1,0:T(8,128)(2,1)S(1)}, u32[]{:S(2)}, u32[]{:S(2)}) collective-permute-start(bf16[100,896]{1,0:T(8,128)(2,1)S(1)} %broadcast_select_fusion.3.refs_8_), channel_id=1, source_target_pairs={{0,4},{2,6},{4,0},{6,2},{8,12},{10,14},{12,8},{14,10},{16,20},{18,... | collective-permute-start | bytes 537608 | tf_op jit(solution)/shard_map/ppermute | solution.py:44
  56.6 8.9 %collective-permute-start.15 = (bf16[100,896]{1,0:T(8,128)(2,1)S(1)}, bf16[100,896]{1,0:T(8,128)(2,1)S(1)}, u32[]{:S(2)}, u32[]{:S(2)}) collective-permute-start(bf16[100,896]{1,0:T(8,128)(2,1)S(1)} %broadcast_select_fusion.2.refs_12_), channel_id=1, source_target_pairs={{0,4},{2,6},{4,0},{6,2},{8,12},{10,14},{12,8},{14,10},{16,20},{18,... | collective-permute-start | bytes 537608 | tf_op jit(solution)/shard_map/ppermute | solution.py:44
  58.2 16.5 %collective-permute-start.22 = (bf16[120,1792]{1,0:T(8,128)(2,1)S(1)}, bf16[120,1792]{1,0:T(8,128)(2,1)S(1)}, u32[]{:S(2)}, u32[]{:S(2)}) collective-permute-start(bf16[120,1792]{1,0:T(8,128)(2,1)S(1)} %collective-permute-done.20.refs_4_), channel_id=1, source_target_pairs={{0,4},{2,6},{4,0},{6,2},{8,12},{10,14},{12,8},{14,10},{16,20},{18,... | collective-permute-start | bytes 1290248 | tf_op jit(solution)/shard_map/ppermute | solution.py:44
  58.8 15.9 %collective-permute-start.21 = (bf16[120,1792]{1,0:T(8,128)(2,1)S(1)}, bf16[120,1792]{1,0:T(8,128)(2,1)S(1)}, u32[]{:S(2)}, u32[]{:S(2)}) collective-permute-start(bf16[120,1792]{1,0:T(8,128)(2,1)S(1)} %collective-permute-done.20.refs_4_), channel_id=1, source_target_pairs={{0,2},{2,0},{4,6},{6,4},{8,10},{10,8},{12,14},{14,12},{16,18},{18,... | collective-permute-start | bytes 1290248 | tf_op jit(solution)/shard_map/ppermute | solution.py:44
  58.8 16.4 %collective-permute-start.19 = (bf16[120,1792]{1,0:T(8,128)(2,1)S(1)}, bf16[120,1792]{1,0:T(8,128)(2,1)S(1)}, u32[]{:S(2)}, u32[]{:S(2)}) collective-permute-start(bf16[120,1792]{1,0:T(8,128)(2,1)S(1)} %collective-permute-done.18.refs_2_), channel_id=1, source_target_pairs={{0,2},{2,0},{4,6},{6,4},{8,10},{10,8},{12,14},{14,12},{16,18},{18,... | collective-permute-start | bytes 1290248 | tf_op jit(solution)/shard_map/ppermute | solution.py:44
  61.5 22.4 %collective-permute-start.27 = (bf16[120,1792]{1,0:T(8,128)(2,1)S(1)}, bf16[120,1792]{1,0:T(8,128)(2,1)S(1)}, u32[]{:S(2)}, u32[]{:S(2)}) collective-permute-start(bf16[120,1792]{1,0:T(8,128)(2,1)S(1)} %broadcast_select_fusion.1.refs_8_), channel_id=1, source_target_pairs={{0,4},{2,6},{4,0},{6,2},{8,12},{10,14},{12,8},{14,10},{16,20},{18,... | collective-permute-start | bytes 1290248 | tf_op jit(solution)/shard_map/ppermute | solution.py:44
  65.5 26.3 %collective-permute-start.32 = (bf16[120,1792]{1,0:T(8,128)(2,1)S(1)}, bf16[120,1792]{1,0:T(8,128)(2,1)S(1)}, u32[]{:S(2)}, u32[]{:S(2)}) collective-permute-start(bf16[120,1792]{1,0:T(8,128)(2,1)S(1)} %broadcast_select_fusion.refs_12_), channel_id=1, source_target_pairs={{0,4},{2,6},{4,0},{6,2},{8,12},{10,14},{12,8},{14,10},{16,20},{18,... | collective-permute-start | bytes 1290248 | tf_op jit(solution)/shard_map/ppermute | solution.py:44
  74.7 18.4 %collective-permute-start.26 = (bf16[120,1792]{1,0:T(8,128)(2,1)S(1)}, bf16[120,1792]{1,0:T(8,128)(2,1)S(1)}, u32[]{:S(2)}, u32[]{:S(2)}) collective-permute-start(bf16[120,1792]{1,0:T(8,128)(2,1)S(1)} %broadcast_select_fusion.1.refs_8_), channel_id=1, source_target_pairs={{0,2},{2,0},{4,6},{6,4},{8,10},{10,8},{12,14},{14,12},{16,18},{18,... | collective-permute-start | bytes 1290248 | tf_op jit(solution)/shard_map/ppermute | solution.py:44
  74.7 19.0 %collective-permute-start.23 = (bf16[120,1792]{1,0:T(8,128)(2,1)S(1)}, bf16[120,1792]{1,0:T(8,128)(2,1)S(1)}, u32[]{:S(2)}, u32[]{:S(2)}) collective-permute-start(bf16[120,1792]{1,0:T(8,128)(2,1)S(1)} %collective-permute-done.22.refs_6_), channel_id=1, source_target_pairs={{0,2},{2,0},{4,6},{6,4},{8,10},{10,8},{12,14},{14,12},{16,18},{18,... | collective-permute-start | bytes 1290248 | tf_op jit(solution)/shard_map/ppermute | solution.py:44
  75.2 18.6 %collective-permute-start.31 = (bf16[120,1792]{1,0:T(8,128)(2,1)S(1)}, bf16[120,1792]{1,0:T(8,128)(2,1)S(1)}, u32[]{:S(2)}, u32[]{:S(2)}) collective-permute-start(bf16[120,1792]{1,0:T(8,128)(2,1)S(1)} %broadcast_select_fusion.refs_12_), channel_id=1, source_target_pairs={{0,2},{2,0},{4,6},{6,4},{8,10},{10,8},{12,14},{14,12},{16,18},{18,... | collective-permute-start | bytes 1290248 | tf_op jit(solution)/shard_map/ppermute | solution.py:44
  83.9 10.3 %collective-permute-start.28 = (bf16[120,1792]{1,0:T(8,128)(2,1)S(1)}, bf16[120,1792]{1,0:T(8,128)(2,1)S(1)}, u32[]{:S(2)}, u32[]{:S(2)}) collective-permute-start(bf16[120,1792]{1,0:T(8,128)(2,1)S(1)} %collective-permute-done.27.refs_10_), channel_id=1, source_target_pairs={{0,2},{2,0},{4,6},{6,4},{8,10},{10,8},{12,14},{14,12},{16,18},{18,... | collective-permute-start | bytes 1290248 | tf_op jit(solution)/shard_map/ppermute | solution.py:44
  91.8 2.5 %collective-permute-start.33 = (bf16[120,1792]{1,0:T(8,128)(2,1)S(1)}, bf16[120,1792]{1,0:T(8,128)(2,1)S(1)}, u32[]{:S(2)}, u32[]{:S(2)}) collective-permute-start(bf16[120,1792]{1,0:T(8,128)(2,1)S(1)} %collective-permute-done.32.refs_14_), channel_id=1, source_target_pairs={{0,2},{2,0},{4,6},{6,4},{8,10},{10,8},{12,14},{14,12},{16,18},{18,... | collective-permute-start | bytes 1290248 | tf_op jit(solution)/shard_map/ppermute | solution.py:44
  93.2 7.0 %collective-permute-start.9 = (bf16[100,896]{1,0:T(8,128)(2,1)S(1)}, bf16[100,896]{1,0:T(8,128)(2,1)S(1)}, u32[]{:S(2)}, u32[]{:S(2)}) collective-permute-start(bf16[100,896]{1,0:T(8,128)(2,1)S(1)} %broadcast_select_fusion.3.refs_8_), channel_id=1, source_target_pairs={{0,2},{2,0},{4,6},{6,4},{8,10},{10,8},{12,14},{14,12},{16,18},{18,... | collective-permute-start | bytes 537608 | tf_op jit(solution)/shard_map/ppermute | solution.py:44
  93.7 6.4 %collective-permute-start.6 = (bf16[100,896]{1,0:T(8,128)(2,1)S(1)}, bf16[100,896]{1,0:T(8,128)(2,1)S(1)}, u32[]{:S(2)}, u32[]{:S(2)}) collective-permute-start(bf16[100,896]{1,0:T(8,128)(2,1)S(1)} %collective-permute-done.5.refs_6_), channel_id=1, source_target_pairs={{0,2},{2,0},{4,6},{6,4},{8,10},{10,8},{12,14},{14,12},{16,18},{18,... | collective-permute-start | bytes 537608 | tf_op jit(solution)/shard_map/ppermute | solution.py:44
  93.8 6.3 %collective-permute-start.14 = (bf16[100,896]{1,0:T(8,128)(2,1)S(1)}, bf16[100,896]{1,0:T(8,128)(2,1)S(1)}, u32[]{:S(2)}, u32[]{:S(2)}) collective-permute-start(bf16[100,896]{1,0:T(8,128)(2,1)S(1)} %broadcast_select_fusion.2.refs_12_), channel_id=1, source_target_pairs={{0,2},{2,0},{4,6},{6,4},{8,10},{10,8},{12,14},{14,12},{16,18},{18,... | collective-permute-start | bytes 537608 | tf_op jit(solution)/shard_map/ppermute | solution.py:44
  94.3 5.9 %collective-permute-start.11 = (bf16[100,896]{1,0:T(8,128)(2,1)S(1)}, bf16[100,896]{1,0:T(8,128)(2,1)S(1)}, u32[]{:S(2)}, u32[]{:S(2)}) collective-permute-start(bf16[100,896]{1,0:T(8,128)(2,1)S(1)} %collective-permute-done.10.refs_10_), channel_id=1, source_target_pairs={{0,2},{2,0},{4,6},{6,4},{8,10},{10,8},{12,14},{14,12},{16,18},{18,... | collective-permute-start | bytes 537608 | tf_op jit(solution)/shard_map/ppermute | solution.py:44
  94.3 5.8 %collective-permute-start.16 = (bf16[100,896]{1,0:T(8,128)(2,1)S(1)}, bf16[100,896]{1,0:T(8,128)(2,1)S(1)}, u32[]{:S(2)}, u32[]{:S(2)}) collective-permute-start(bf16[100,896]{1,0:T(8,128)(2,1)S(1)} %collective-permute-done.15.refs_14_), channel_id=1, source_target_pairs={{0,2},{2,0},{4,6},{6,4},{8,10},{10,8},{12,14},{14,12},{16,18},{18,... | collective-permute-start | bytes 537608 | tf_op jit(solution)/shard_map/ppermute | solution.py:44
  94.8 5.4 %copy-start.4 = (s32[8]{0:T(128)S(1)}, s32[8]{0:T(128)}, u32[]{:S(2)}) copy-start(s32[8]{0:T(128)} %refs_16_.1) | copy-start | bytes 100
  98.7 1.4 %copy-start.5 = (f32[7,640,128]{2,1,0:T(8,128)}, f32[7,640,128]{2,1,0:T(8,128)S(1)}, u32[]{:S(2)}) copy-start(f32[7,640,128]{2,1,0:T(8,128)S(1)} %get-tuple-element.14.refs_18_) | copy-start | bytes 6881284
  100.2 1.6 %copy-start.6 = (f32[7,640,128]{2,1,0:T(8,128)S(1)}, f32[7,640,128]{2,1,0:T(8,128)}, u32[]{:S(2)}) copy-start(f32[7,640,128]{2,1,0:T(8,128)} %copy-done.5) | copy-start | bytes 6881284
  115.6 8.4 %collective-permute-start.35 = (bf16[8,16,1024]{2,1,0:T(8,128)(2,1)S(1)}, bf16[8,16,1024]{2,1,0:T(8,128)(2,1)S(1)}, u32[]{:S(2)}, u32[]{:S(2)}) collective-permute-start(bf16[8,16,1024]{2,1,0:T(8,128)(2,1)S(1)} %bitcast.37), channel_id=1, source_target_pairs={{0,1},{1,0},{2,3},{3,2},{4,5},{5,4},{6,7},{7,6},{8,9},{9,8},{10,11... | collective-permute-start | bytes 786440 | tf_op jit(solution)/shard_map/ppermute | solution.py:362
  124.0 0.8 copy-start.7
where the time goes:
time: 125 us
  waiting for transfers between devices  60.1 us (48%)
  starting transfers between devices  32.7 us (26%)
  Pallas kernels  23.7 us (19%)
  local copies, waits for them, and re-layouts  4.06 us (3%)
  other arithmetic  2.21 us (2%)
    ppermute x34, waiting for transfers between devices, move(): return lax.ppermute(array, 'dp', pairs)  58.2 us
    ppermute x34, starting transfers between devices, move(): return lax.ppermute(array, 'dp', pairs)  29.6 us
    pallas_call x1, Pallas kernels, shards(): pl.pallas_call(functools.partial(attend_kernel, count, clips, frames), na...  13.7 us
    pallas_call x1, Pallas kernels, shards(): pl.pallas_call(text_grad_kernel, name='text_grad', out_shape=jax.ShapeDty...  4.79 us
    pallas_call x1, Pallas kernels, shards(): pl.pallas_call(functools.partial(project_kernel, count, out_rows), name='...  3.93 us
    unnamed x18, local copies, waits for them, and re-layouts  3.88 us
  transfers between devices with their start and end apart: 36, of which 10 were waited for; matrix products, arithmetic and copies ran while one was open for 3% of the time, Pallas kernels for 8%

commit v1 on v0

--- a/solution.py
+++ b/solution.py
@@ -39,7 +39,7 @@
     return count // 4 == 4
 
 
-def pieces_of(own, count):
+def pieces_of(own, count, tag):
     def move(array, pairs):
         return lax.ppermute(array, "dp", pairs)
 
@@ -50,6 +50,7 @@
         return [(i, i ^ mask) for i in range(count)]
 
     pieces = {0: own}
+    parts = {}
     if relayed(count):
         place = lax.axis_index("dp") // 4
         inner = (place == 1) | (place == 2)
@@ -57,13 +58,20 @@
         pieces[4] = move(own, flip(4))
         first = move(own, swap)
         second = move(pieces[4], swap)
-        pieces[8] = jnp.where(inner, first, move(first, ends))
-        pieces[12] = jnp.where(inner, second, move(second, ends))
+        parts = {8: (first, move(first, ends)), 12: (second, move(second, ends))}
+        for mask, (near, far) in parts.items():
+            pieces[mask] = jnp.where(inner, near, far)
     else:
         for mask in range(4, count, 4):
             pieces[mask] = move(own, flip(mask))
     for mask in range(0, count, 4):
-        if mask + 2 < count:
+        if mask in parts and tag == "p":
+            near, far = parts[mask]
+            middle = [(i, j) for i, j in flip(2) if i // 4 in (1, 2)]
+            outer = [(i, j) for i, j in flip(2) if i // 4 not in (1, 2)]
+            near = move(near, middle)
+            pieces[mask + 2] = jnp.where(inner, near, move(far, outer))
+        elif mask + 2 < count:
             pieces[mask + 2] = move(pieces[mask], flip(2))
     for mask in range(0, count, 2):
         pieces[mask + 1] = move(pieces[mask], flip(1))
@@ -281,8 +289,8 @@
         ],
         0,
     )
-    packs = pieces_of(pack, count)
-    query_pieces = pieces_of(query_weight, count)
+    packs = pieces_of(pack, count, "p")
+    query_pieces = pieces_of(query_weight, count, "q")
 
     pooled = jnp.einsum(
         "flp,cfpv->cflv", pool_weight, video_tokens, preferred_element_type=F32

time: 125 us -> 139 us (1.11)
  waiting for transfers between devices: 60.1 us -> 68.1 us
  starting transfers between devices: 32.7 us -> 38 us
    ppermute x34 -> x36, waiting for transfers between devices: 58.2 us -> 66.2 us  [move(): return lax.ppermute(array, 'dp', pairs)]
    ppermute x34 -> x36, starting transfers between devices: 29.6 us -> 34.9 us  [move(): return lax.ppermute(array, 'dp', pairs)]
  transfers between devices with their start and end apart: 36 -> 38, of which waited for: 10 -> 11; matrix products, arithmetic and copies ran while one was open for 3% -> 2% of each run, Pallas kernels for 8% -> 7%
where the time goes in v1:
time: 139 us; the launch traced here: 138 us
  waiting for transfers between devices  68.1 us (49%)
  starting transfers between devices  38 us (27%)
  Pallas kernels  23.7 us (17%)
  local copies, waits for them, and re-layouts  4.05 us (3%)
  other arithmetic  2.32 us (2%)
    ppermute x36, waiting for transfers between devices, move(): return lax.ppermute(array, 'dp', pairs)  66.2 us
    ppermute x36, starting transfers between devices, move(): return lax.ppermute(array, 'dp', pairs)  34.9 us
    pallas_call x1, Pallas kernels, shards(): pl.pallas_call(functools.partial(attend_kernel, count, clips, frames), na...  13.7 us
    pallas_call x1, Pallas kernels, shards(): pl.pallas_call(text_grad_kernel, name='text_grad', out_shape=jax.ShapeDty...  4.79 us
    pallas_call x1, Pallas kernels, shards(): pl.pallas_call(functools.partial(project_kernel, count, out_rows), name='...  3.91 us
    unnamed x18, local copies, waits for them, and re-layouts  3.87 us
  transfers between devices with their start and end apart: 38, of which 11 were waited for; matrix products, arithmetic and copies ran while one was open for 2% of the time, Pallas kernels for 7%

profile of v1, /device:TPU:0, one launch (start us, length us, event | category | flops | bytes accessed | tf_op | source)
XLA Modules:
  0.0 138.2 jit_solution(4569403655957557944)
XLA Ops:
  0.6 0.0 copy-start
  0.6 0.0 copy-start.3
  0.7 3.1 %collective-permute-start.3 = (bf16[100,896]{1,0:T(8,128)(2,1)}, bf16[100,896]{1,0:T(8,128)(2,1)S(1)}, u32[]{:S(2)}, u32[]{:S(2)}) collective-permute-start(bf16[100,896]{1,0:T(8,128)(2,1)} %refs_0_.1), channel_id=1, source_target_pairs={{0,8},{2,10},{4,12},{6,14},{8,0},{10,2},{12,4},{14,6},{16,24},{18,... | collective-permute-start | bytes 537608 | tf_op jit(solution)/shard_map/ppermute | solution.py:44
  3.8 1.3 collective-permute-start.7
  5.1 1.1 fusion.2.refs_0_
  6.2 3.8 %collective-permute-start.20 = (bf16[120,1792]{1,0:T(8,128)(2,1)S(1)}, bf16[120,1792]{1,0:T(8,128)(2,1)S(1)}, u32[]{:S(2)}, u32[]{:S(2)}) collective-permute-start(bf16[120,1792]{1,0:T(8,128)(2,1)S(1)} %fusion.2.refs_0_), channel_id=1, source_target_pairs={{0,8},{2,10},{4,12},{6,14},{8,0},{10,2},{12,4},{14,6},{16,24},{18,... | collective-permute-start | bytes 1290248 | tf_op jit(solution)/shard_map/ppermute | solution.py:44
  10.0 0.7 collective-permute-start.24
  10.7 1.6 %collective-permute-start.1 = (bf16[100,896]{1,0:T(8,128)(2,1)}, bf16[100,896]{1,0:T(8,128)(2,1)S(1)}, u32[]{:S(2)}, u32[]{:S(2)}) collective-permute-start(bf16[100,896]{1,0:T(8,128)(2,1)} %refs_0_.1), channel_id=1, source_target_pairs={{0,4},{2,6},{4,0},{6,2},{8,12},{10,14},{12,8},{14,10},{16,20},{18,... | collective-permute-start | bytes 537608 | tf_op jit(solution)/shard_map/ppermute | solution.py:44
  12.2 0.0 collective-permute-done.3.refs_4_
  12.2 1.3 collective-permute-start.12
  13.6 1.3 collective-permute-start.8
  14.9 1.0 convolution_convert_fusion
  16.0 0.1 collective-permute-start
  16.0 7.4 %collective-permute-done.8 = bf16[100,896]{1,0:T(8,128)(2,1)} collective-permute-done((bf16[100,896]{1,0:T(8,128)(2,1)}, bf16[100,896]{1,0:T(8,128)(2,1)}, u32[]{:S(2)}, u32[]{:S(2)}) %collective-permute-start.8) | collective-permute-done | bytes 179232 | tf_op jit(solution)/shard_map/ppermute | solution.py:44
  23.4 1.3 collective-permute-start.13
  24.7 0.7 collective-permute-start.30
  25.4 1.3 collective-permute-start.25
  26.7 1.0 broadcast_select_fusion.5.refs_8_
  27.7 6.2 %collective-permute-done.13 = bf16[100,896]{1,0:T(8,128)(2,1)S(1)} collective-permute-done((bf16[100,896]{1,0:T(8,128)(2,1)}, bf16[100,896]{1,0:T(8,128)(2,1)S(1)}, u32[]{:S(2)}, u32[]{:S(2)}) %collective-permute-start.13) | collective-permute-done | bytes 179232 | tf_op jit(solution)/shard_map/ppermute | solution.py:44
  33.9 1.5 %collective-permute-start.36 = (bf16[128,1024]{1,0:T(8,128)(2,1)S(1)}, bf16[128,1024]{1,0:T(8,128)(2,1)S(1)}, u32[]{:S(2)}, u32[]{:S(2)}) collective-permute-start(bf16[128,1024]{1,0:T(8,128)(2,1)S(1)} %get-tuple-element.23), channel_id=1, source_target_pairs={{0,1},{1,0},{2,3},{3,2},{4,5},{5,4},{6,7},{7,6},{8,9},{9,8},{10,11... | collective-permute-start | bytes 786440 | tf_op jit(solution)/shard_map/ppermute | solution.py:303
  35.5 1.6 %collective-permute-start.5 = (bf16[100,896]{1,0:T(8,128)(2,1)S(1)}, bf16[100,896]{1,0:T(8,128)(2,1)S(1)}, u32[]{:S(2)}, u32[]{:S(2)}) collective-permute-start(bf16[100,896]{1,0:T(8,128)(2,1)S(1)} %collective-permute-done.3.refs_4_), channel_id=1, source_target_pairs={{0,4},{2,6},{4,0},{6,2},{8,12},{10,14},{12,8},{14,10},{16,20},{18,... | collective-permute-start | bytes 537608 | tf_op jit(solution)/shard_map/ppermute | solution.py:44
  37.0 6.3 %collective-permute-done.25 = bf16[120,1792]{1,0:T(8,128)(2,1)S(1)} collective-permute-done((bf16[120,1792]{1,0:T(8,128)(2,1)S(1)}, bf16[120,1792]{1,0:T(8,128)(2,1)S(1)}, u32[]{:S(2)}, u32[]{:S(2)}) %collective-permute-start.25) | collective-permute-done | bytes 430112 | tf_op jit(solution)/shard_map/ppermute | solution.py:44
  43.3 1.3 collective-permute-start.31
  44.6 0.1 broadcast_select_fusion.3.refs_8_
  44.6 0.0 copy-start.8
  44.7 0.0 copy-start.1
  44.7 0.1 collective-permute-start.4
  44.8 0.8 collective-permute-start.27
  45.6 11.0 %collective-permute-done.31 = bf16[120,1792]{1,0:T(8,128)(2,1)S(1)} collective-permute-done((bf16[120,1792]{1,0:T(8,128)(2,1)S(1)}, bf16[120,1792]{1,0:T(8,128)(2,1)S(1)}, u32[]{:S(2)}, u32[]{:S(2)}) %collective-permute-start.31) | collective-permute-done | bytes 430112 | tf_op jit(solution)/shard_map/ppermute | solution.py:44
  56.6 3.4 %collective-permute-start.28 = (bf16[120,1792]{1,0:T(8,128)(2,1)S(1)}, bf16[120,1792]{1,0:T(8,128)(2,1)S(1)}, u32[]{:S(2)}, u32[]{:S(2)}) collective-permute-start(bf16[120,1792]{1,0:T(8,128)(2,1)S(1)} %collective-permute-done.25), channel_id=1, source_target_pairs={{0,4},{2,6},{4,0},{6,2},{24,28},{26,30},{28,24},{30,26},{1,5},{3,7... | collective-permute-start | bytes 1290248 | tf_op jit(solution)/shard_map/ppermute | solution.py:44
  60.0 0.1 broadcast_select_fusion.1.refs_12_
  60.1 0.6 collective-permute-start.18
  60.7 0.5 collective-permute-start.2
  61.2 0.7 collective-permute-start.33
  61.9 9.4 %collective-permute-done.28 = bf16[120,1792]{1,0:T(8,128)(2,1)S(1)} collective-permute-done((bf16[120,1792]{1,0:T(8,128)(2,1)S(1)}, bf16[120,1792]{1,0:T(8,128)(2,1)S(1)}, u32[]{:S(2)}, u32[]{:S(2)}) %collective-permute-start.28) | collective-permute-done | bytes 430112 | tf_op jit(solution)/shard_map/ppermute | solution.py:44
  71.3 3.4 %collective-permute-start.34 = (bf16[120,1792]{1,0:T(8,128)(2,1)S(1)}, bf16[120,1792]{1,0:T(8,128)(2,1)S(1)}, u32[]{:S(2)}, u32[]{:S(2)}) collective-permute-start(bf16[120,1792]{1,0:T(8,128)(2,1)S(1)} %collective-permute-done.31), channel_id=1, source_target_pairs={{0,4},{2,6},{4,0},{6,2},{24,28},{26,30},{28,24},{30,26},{1,5},{3,7... | collective-permute-start | bytes 1290248 | tf_op jit(solution)/shard_map/ppermute | solution.py:44
  74.7 0.0 copy-start.2
  74.8 0.6 collective-permute-start.10
  75.4 5.1 %collective-permute-done.18.refs_2_ = bf16[120,1792]{1,0:T(8,128)(2,1)S(1)} collective-permute-done((bf16[120,1792]{1,0:T(8,128)(2,1)S(1)}, bf16[120,1792]{1,0:T(8,128)(2,1)S(1)}, u32[]{:S(2)}, u32[]{:S(2)}) %collective-permute-start.18) | collective-permute-done | bytes 430112 | tf_op jit(solution)/shard_map/ppermute | solution.py:44
  80.5 1.5 %collective-permute-start.22 = (bf16[120,1792]{1,0:T(8,128)(2,1)S(1)}, bf16[120,1792]{1,0:T(8,128)(2,1)S(1)}, u32[]{:S(2)}, u32[]{:S(2)}) collective-permute-start(bf16[120,1792]{1,0:T(8,128)(2,1)S(1)} %collective-permute-done.20.refs_4_), channel_id=1, source_target_pairs={{0,4},{2,6},{4,0},{6,2},{8,12},{10,14},{12,8},{14,10},{16,20},{18,... | collective-permute-start | bytes 1290248 | tf_op jit(solution)/shard_map/ppermute | solution.py:44
  82.0 0.5 collective-permute-start.19
  82.5 7.2 %collective-permute-done.34 = bf16[120,1792]{1,0:T(8,128)(2,1)S(1)} collective-permute-done((bf16[120,1792]{1,0:T(8,128)(2,1)S(1)}, bf16[120,1792]{1,0:T(8,128)(2,1)S(1)}, u32[]{:S(2)}, u32[]{:S(2)}) %collective-permute-start.34) | collective-permute-done | bytes 430112 | tf_op jit(solution)/shard_map/ppermute | solution.py:44
  89.7 1.5 %collective-permute-start.15 = (bf16[100,896]{1,0:T(8,128)(2,1)S(1)}, bf16[100,896]{1,0:T(8,128)(2,1)S(1)}, u32[]{:S(2)}, u32[]{:S(2)}) collective-permute-start(bf16[100,896]{1,0:T(8,128)(2,1)S(1)} %broadcast_select_fusion.4.refs_12_), channel_id=1, source_target_pairs={{0,4},{2,6},{4,0},{6,2},{8,12},{10,14},{12,8},{14,10},{16,20},{18,... | collective-permute-start | bytes 537608 | tf_op jit(solution)/shard_map/ppermute | solution.py:44
  91.3 2.5 %collective-permute-done.10.refs_10_ = bf16[100,896]{1,0:T(8,128)(2,1)S(1)} collective-permute-done((bf16[100,896]{1,0:T(8,128)(2,1)S(1)}, bf16[100,896]{1,0:T(8,128)(2,1)S(1)}, u32[]{:S(2)}, u32[]{:S(2)}) %collective-permute-start.10) | collective-permute-done | bytes 179232 | tf_op jit(solution)/shard_map/ppermute | solution.py:44
  93.7 9.0 %collective-permute-done.22.refs_6_ = bf16[120,1792]{1,0:T(8,128)(2,1)S(1)} collective-permute-done((bf16[120,1792]{1,0:T(8,128)(2,1)S(1)}, bf16[120,1792]{1,0:T(8,128)(2,1)S(1)}, u32[]{:S(2)}, u32[]{:S(2)}) %collective-permute-start.22) | collective-permute-done | bytes 430112 | tf_op jit(solution)/shard_map/ppermute | solution.py:44
  102.7 2.0 %collective-permute-done.15.refs_14_ = bf16[100,896]{1,0:T(8,128)(2,1)S(1)} collective-permute-done((bf16[100,896]{1,0:T(8,128)(2,1)S(1)}, bf16[100,896]{1,0:T(8,128)(2,1)S(1)}, u32[]{:S(2)}, u32[]{:S(2)}) %collective-permute-start.15) | collective-permute-done | bytes 179232 | tf_op jit(solution)/shard_map/ppermute | solution.py:44
  104.7 0.5 collective-permute-start.32
  105.3 0.1 collective-permute-start.35
  105.3 1.3 norm.1
  106.7 0.5 collective-permute-start.9
  107.2 0.1 collective-permute-start.6
  107.3 0.4 collective-permute-start.14
  107.7 0.1 collective-permute-start.11
  107.8 0.4 collective-permute-start.16
  108.2 3.9 %project.1 = (bf16[256,1792]{1,0:T(8,128)(2,1)S(1)}, bf16[1024,1792]{1,0:T(8,128)(2,1)S(1)}, f32[7,640,128]{2,1,0:T(8,128)S(1)}) custom-call(bf16[120,1792]{1,0:T(8,128)(2,1)S(1)} %fusion.2.refs_0_, bf16[120,1792]{1,0:T(8,128)(2,1)S(1)} %collective-permute-done.17.refs_1_, bf16[120,1792]{1,0:T(8,128)(2,1)S(1)} %collective-permute-done.18.refs_2_, ...), custom_call_target="tpu_custom_call" | custom-call | flops 2705719296 | bytes 9404416 | tf_op jit(solution)/shard_map/project/pallas_call | solution.py:325
  112.2 1.4 %copy-done.5 = f32[7,640,128]{2,1,0:T(8,128)} copy-done((f32[7,640,128]{2,1,0:T(8,128)}, f32[7,640,128]{2,1,0:T(8,128)S(1)}, u32[]{:S(2)}) %copy-start.5) | copy-done | bytes 2293784
  113.6 1.6 %copy-done.6 = f32[7,640,128]{2,1,0:T(8,128)S(1)} copy-done((f32[7,640,128]{2,1,0:T(8,128)S(1)}, f32[7,640,128]{2,1,0:T(8,128)}, u32[]{:S(2)}) %copy-start.6) | copy-done | bytes 2293784
  115.2 13.7 %attend.1 = (bf16[616,896]{1,0:T(8,128)(2,1)S(1)}, bf16[256,1024]{1,0:T(8,128)(2,1)S(1)}, bf16[1600,896]{1,0:T(8,128)(2,1)S(1)}) custom-call(bf16[100,896]{1,0:T(8,128)(2,1)S(1)} %copy-done.3, bf16[100,896]{1,0:T(8,128)(2,1)S(1)} %collective-permute-done.refs_1_, bf16[100,896]{1,0:T(8,128)(2,1)S(1)} %collective-permute-done.1.refs_2_, ...), custom_call_target="tpu_custom_call" | custom-call | flops 3532390400 | bytes 11468800 | tf_op jit(solution)/shard_map/attend/pallas_call | solution.py:346
  129.0 1.6 %collective-permute-start.37 = (bf16[8,16,1024]{2,1,0:T(8,128)(2,1)S(1)}, bf16[8,16,1024]{2,1,0:T(8,128)(2,1)S(1)}, u32[]{:S(2)}, u32[]{:S(2)}) collective-permute-start(bf16[8,16,1024]{2,1,0:T(8,128)(2,1)S(1)} %bitcast.37), channel_id=1, source_target_pairs={{0,1},{1,0},{2,3},{3,2},{4,5},{5,4},{6,7},{7,6},{8,9},{9,8},{10,11... | collective-permute-start | bytes 786440 | tf_op jit(solution)/shard_map/ppermute | solution.py:370
  130.6 0.1 broadcast_in_dim.8
  130.7 4.8 %text_grad.1 = bf16[616,1600]{1,0:T(8,128)(2,1)} custom-call(bf16[616,1600]{1,0:T(8,128)(2,1)S(1)} %bitcast.31, f32[616,128]{1,0:T(8,128)S(1)} %get-tuple-element.11.mean_ref, f32[616,128]{1,0:T(8,128)S(1)} %get-tuple-element.12.inv_ref, f32[1,1600]{1,0:T(1,128)S(1)} %reshape.35.gain_ref, bf16[616,896]{1,0:T(8,128)(2,1)S(1)} %get-tuple-element.17.gq_ref, ...), custom_call_target="tpu_custom_call" | custom-call | flops 1766195200 | bytes 6809600 | tf_op jit(solution)/shard_map/text_grad/pallas_call | solution.py:378
  135.5 1.9 %collective-permute-done.37 = bf16[8,16,1024]{2,1,0:T(8,128)(2,1)S(1)} collective-permute-done((bf16[8,16,1024]{2,1,0:T(8,128)(2,1)S(1)}, bf16[8,16,1024]{2,1,0:T(8,128)(2,1)S(1)}, u32[]{:S(2)}, u32[]{:S(2)}) %collective-permute-start.37) | collective-permute-done | bytes 262176 | tf_op jit(solution)/shard_map/ppermute | solution.py:370
  137.4 0.0 copy-start.7
  137.4 0.8 copy-done.7
  (49 shorter events, 0.4 us)
Async XLA Ops:
  0.6 14.2 %copy-start = (bf16[16,1,32,1024]{3,2,1,0:T(8,128)(2,1)S(1)}, bf16[16,1,32,1024]{3,2,1,0:T(8,128)(2,1)}, u32[]{:S(2)}) copy-start(bf16[16,1,32,1024]{3,2,1,0:T(8,128)(2,1)} %param.10) | copy-start | bytes 3145732
  0.6 15.3 %copy-start.3 = (bf16[100,896]{1,0:T(8,128)(2,1)S(1)}, bf16[100,896]{1,0:T(8,128)(2,1)}, u32[]{:S(2)}) copy-start(bf16[100,896]{1,0:T(8,128)(2,1)} %refs_0_.1) | copy-start | bytes 537604
  0.7 11.6 %collective-permute-start.3 = (bf16[100,896]{1,0:T(8,128)(2,1)}, bf16[100,896]{1,0:T(8,128)(2,1)S(1)}, u32[]{:S(2)}, u32[]{:S(2)}) collective-permute-start(bf16[100,896]{1,0:T(8,128)(2,1)} %refs_0_.1), channel_id=1, source_target_pairs={{0,8},{2,10},{4,12},{6,14},{8,0},{10,2},{12,4},{14,6},{16,24},{18,... | collective-permute-start | bytes 537608 | tf_op jit(solution)/shard_map/ppermute | solution.py:44
  3.8 9.8 %collective-permute-start.7 = (bf16[100,896]{1,0:T(8,128)(2,1)}, bf16[100,896]{1,0:T(8,128)(2,1)}, u32[]{:S(2)}, u32[]{:S(2)}) collective-permute-start(bf16[100,896]{1,0:T(8,128)(2,1)} %refs_0_.1), channel_id=1, source_target_pairs={{8,16},{10,18},{12,20},{14,22},{16,8},{18,10},{20,12},{22,14},{9,1... | collective-permute-start | bytes 537608 | tf_op jit(solution)/shard_map/ppermute | solution.py:44
  6.2 18.5 %collective-permute-start.20 = (bf16[120,1792]{1,0:T(8,128)(2,1)S(1)}, bf16[120,1792]{1,0:T(8,128)(2,1)S(1)}, u32[]{:S(2)}, u32[]{:S(2)}) collective-permute-start(bf16[120,1792]{1,0:T(8,128)(2,1)S(1)} %fusion.2.refs_0_), channel_id=1, source_target_pairs={{0,8},{2,10},{4,12},{6,14},{8,0},{10,2},{12,4},{14,6},{16,24},{18,... | collective-permute-start | bytes 1290248 | tf_op jit(solution)/shard_map/ppermute | solution.py:44
  10.0 15.4 %collective-permute-start.24 = (bf16[120,1792]{1,0:T(8,128)(2,1)S(1)}, bf16[120,1792]{1,0:T(8,128)(2,1)S(1)}, u32[]{:S(2)}, u32[]{:S(2)}) collective-permute-start(bf16[120,1792]{1,0:T(8,128)(2,1)S(1)} %fusion.2.refs_0_), channel_id=1, source_target_pairs={{8,16},{10,18},{12,20},{14,22},{16,8},{18,10},{20,12},{22,14},{9,1... | collective-permute-start | bytes 1290248 | tf_op jit(solution)/shard_map/ppermute | solution.py:44
  10.7 34.0 %collective-permute-start.1 = (bf16[100,896]{1,0:T(8,128)(2,1)}, bf16[100,896]{1,0:T(8,128)(2,1)S(1)}, u32[]{:S(2)}, u32[]{:S(2)}) collective-permute-start(bf16[100,896]{1,0:T(8,128)(2,1)} %refs_0_.1), channel_id=1, source_target_pairs={{0,4},{2,6},{4,0},{6,2},{8,12},{10,14},{12,8},{14,10},{16,20},{18,... | collective-permute-start | bytes 537608 | tf_op jit(solution)/shard_map/ppermute | solution.py:44
  12.2 3.7 %collective-permute-start.12 = (bf16[100,896]{1,0:T(8,128)(2,1)S(1)}, bf16[100,896]{1,0:T(8,128)(2,1)}, u32[]{:S(2)}, u32[]{:S(2)}) collective-permute-start(bf16[100,896]{1,0:T(8,128)(2,1)S(1)} %collective-permute-done.3.refs_4_), channel_id=1, source_target_pairs={{8,16},{10,18},{12,20},{14,22},{16,8},{18,10},{20,12},{22,14},{9,1... | collective-permute-start | bytes 537608 | tf_op jit(solution)/shard_map/ppermute | solution.py:44
  13.6 9.9 %collective-permute-start.8 = (bf16[100,896]{1,0:T(8,128)(2,1)}, bf16[100,896]{1,0:T(8,128)(2,1)}, u32[]{:S(2)}, u32[]{:S(2)}) collective-permute-start(bf16[100,896]{1,0:T(8,128)(2,1)} %collective-permute-done.7), channel_id=1, source_target_pairs={{8,0},{10,2},{12,4},{14,6},{16,24},{18,26},{20,28},{22,30},{9,1},{... | collective-permute-start | bytes 537608 | tf_op jit(solution)/shard_map/ppermute | solution.py:44
  16.0 28.8 %collective-permute-start = (bf16[100,896]{1,0:T(8,128)(2,1)S(1)}, bf16[100,896]{1,0:T(8,128)(2,1)S(1)}, u32[]{:S(2)}, u32[]{:S(2)}) collective-permute-start(bf16[100,896]{1,0:T(8,128)(2,1)S(1)} %copy-done.3), channel_id=1, source_target_pairs={{0,2},{2,0},{4,6},{6,4},{8,10},{10,8},{12,14},{14,12},{16,18},{18,... | collective-permute-start | bytes 537608 | tf_op jit(solution)/shard_map/ppermute | solution.py:44
  23.4 10.5 %collective-permute-start.13 = (bf16[100,896]{1,0:T(8,128)(2,1)}, bf16[100,896]{1,0:T(8,128)(2,1)S(1)}, u32[]{:S(2)}, u32[]{:S(2)}) collective-permute-start(bf16[100,896]{1,0:T(8,128)(2,1)} %collective-permute-done.12), channel_id=1, source_target_pairs={{8,0},{10,2},{12,4},{14,6},{16,24},{18,26},{20,28},{22,30},{9,1},{... | collective-permute-start | bytes 537608 | tf_op jit(solution)/shard_map/ppermute | solution.py:44
  24.7 10.7 %collective-permute-start.30 = (bf16[120,1792]{1,0:T(8,128)(2,1)S(1)}, bf16[120,1792]{1,0:T(8,128)(2,1)S(1)}, u32[]{:S(2)}, u32[]{:S(2)}) collective-permute-start(bf16[120,1792]{1,0:T(8,128)(2,1)S(1)} %collective-permute-done.20.refs_4_), channel_id=1, source_target_pairs={{8,16},{10,18},{12,20},{14,22},{16,8},{18,10},{20,12},{22,14},{9,1... | collective-permute-start | bytes 1290248 | tf_op jit(solution)/shard_map/ppermute | solution.py:44
  25.4 17.9 %collective-permute-start.25 = (bf16[120,1792]{1,0:T(8,128)(2,1)S(1)}, bf16[120,1792]{1,0:T(8,128)(2,1)S(1)}, u32[]{:S(2)}, u32[]{:S(2)}) collective-permute-start(bf16[120,1792]{1,0:T(8,128)(2,1)S(1)} %collective-permute-done.24), channel_id=1, source_target_pairs={{8,0},{10,2},{12,4},{14,6},{16,24},{18,26},{20,28},{22,30},{9,1},{... | collective-permute-start | bytes 1290248 | tf_op jit(solution)/shard_map/ppermute | solution.py:44
  33.9 26.2 %collective-permute-start.36 = (bf16[128,1024]{1,0:T(8,128)(2,1)S(1)}, bf16[128,1024]{1,0:T(8,128)(2,1)S(1)}, u32[]{:S(2)}, u32[]{:S(2)}) collective-permute-start(bf16[128,1024]{1,0:T(8,128)(2,1)S(1)} %get-tuple-element.23), channel_id=1, source_target_pairs={{0,1},{1,0},{2,3},{3,2},{4,5},{5,4},{6,7},{7,6},{8,9},{9,8},{10,11... | collective-permute-start | bytes 786440 | tf_op jit(solution)/shard_map/ppermute | solution.py:303
  35.5 25.2 %collective-permute-start.5 = (bf16[100,896]{1,0:T(8,128)(2,1)S(1)}, bf16[100,896]{1,0:T(8,128)(2,1)S(1)}, u32[]{:S(2)}, u32[]{:S(2)}) collective-permute-start(bf16[100,896]{1,0:T(8,128)(2,1)S(1)} %collective-permute-done.3.refs_4_), channel_id=1, source_target_pairs={{0,4},{2,6},{4,0},{6,2},{8,12},{10,14},{12,8},{14,10},{16,20},{18,... | collective-permute-start | bytes 537608 | tf_op jit(solution)/shard_map/ppermute | solution.py:44
  43.3 13.3 %collective-permute-start.31 = (bf16[120,1792]{1,0:T(8,128)(2,1)S(1)}, bf16[120,1792]{1,0:T(8,128)(2,1)S(1)}, u32[]{:S(2)}, u32[]{:S(2)}) collective-permute-start(bf16[120,1792]{1,0:T(8,128)(2,1)S(1)} %collective-permute-done.30), channel_id=1, source_target_pairs={{8,0},{10,2},{12,4},{14,6},{16,24},{18,26},{20,28},{22,30},{9,1},{... | collective-permute-start | bytes 1290248 | tf_op jit(solution)/shard_map/ppermute | solution.py:44
  44.6 60.7 %copy-start.8 = (f32[1600]{0:T(1024)S(1)}, f32[1600]{0:T(1024)}, u32[]{:S(2)}) copy-start(f32[1600]{0:T(1024)} %param.13) | copy-start | bytes 19204
  44.7 60.7 %copy-start.1 = (bf16[8,77,1600]{2,0,1:T(8,128)(2,1)S(1)}, bf16[8,77,1600]{2,0,1:T(8,128)(2,1)}, u32[]{:S(2)}) copy-start(bf16[8,77,1600]{2,0,1:T(8,128)(2,1)} %param.12) | copy-start | bytes 5913604
  44.7 16.0 %collective-permute-start.4 = (bf16[100,896]{1,0:T(8,128)(2,1)S(1)}, bf16[100,896]{1,0:T(8,128)(2,1)S(1)}, u32[]{:S(2)}, u32[]{:S(2)}) collective-permute-start(bf16[100,896]{1,0:T(8,128)(2,1)S(1)} %collective-permute-done.3.refs_4_), channel_id=1, source_target_pairs={{0,2},{2,0},{4,6},{6,4},{8,10},{10,8},{12,14},{14,12},{16,18},{18,... | collective-permute-start | bytes 537608 | tf_op jit(solution)/shard_map/ppermute | solution.py:44
  44.8 16.4 %collective-permute-start.27 = (bf16[120,1792]{1,0:T(8,128)(2,1)S(1)}, bf16[120,1792]{1,0:T(8,128)(2,1)S(1)}, u32[]{:S(2)}, u32[]{:S(2)}) collective-permute-start(bf16[120,1792]{1,0:T(8,128)(2,1)S(1)} %collective-permute-done.24), channel_id=1, source_target_pairs={{8,12},{10,14},{12,8},{14,10},{16,20},{18,22},{20,16},{22,18},{9,1... | collective-permute-start | bytes 1290248 | tf_op jit(solution)/shard_map/ppermute | solution.py:44
  56.6 14.7 %collective-permute-start.28 = (bf16[120,1792]{1,0:T(8,128)(2,1)S(1)}, bf16[120,1792]{1,0:T(8,128)(2,1)S(1)}, u32[]{:S(2)}, u32[]{:S(2)}) collective-permute-start(bf16[120,1792]{1,0:T(8,128)(2,1)S(1)} %collective-permute-done.25), channel_id=1, source_target_pairs={{0,4},{2,6},{4,0},{6,2},{24,28},{26,30},{28,24},{30,26},{1,5},{3,7... | collective-permute-start | bytes 1290248 | tf_op jit(solution)/shard_map/ppermute | solution.py:44
  60.1 20.4 %collective-permute-start.18 = (bf16[120,1792]{1,0:T(8,128)(2,1)S(1)}, bf16[120,1792]{1,0:T(8,128)(2,1)S(1)}, u32[]{:S(2)}, u32[]{:S(2)}) collective-permute-start(bf16[120,1792]{1,0:T(8,128)(2,1)S(1)} %fusion.2.refs_0_), channel_id=1, source_target_pairs={{0,4},{2,6},{4,0},{6,2},{8,12},{10,14},{12,8},{14,10},{16,20},{18,... | collective-permute-start | bytes 1290248 | tf_op jit(solution)/shard_map/ppermute | solution.py:44
  60.7 21.3 %collective-permute-start.17 = (bf16[120,1792]{1,0:T(8,128)(2,1)S(1)}, bf16[120,1792]{1,0:T(8,128)(2,1)S(1)}, u32[]{:S(2)}, u32[]{:S(2)}) collective-permute-start(bf16[120,1792]{1,0:T(8,128)(2,1)S(1)} %fusion.2.refs_0_), channel_id=1, source_target_pairs={{0,2},{2,0},{4,6},{6,4},{8,10},{10,8},{12,14},{14,12},{16,18},{18,... | collective-permute-start | bytes 1290248 | tf_op jit(solution)/shard_map/ppermute | solution.py:44
  60.7 14.0 %collective-permute-start.2 = (bf16[100,896]{1,0:T(8,128)(2,1)S(1)}, bf16[100,896]{1,0:T(8,128)(2,1)S(1)}, u32[]{:S(2)}, u32[]{:S(2)}) collective-permute-start(bf16[100,896]{1,0:T(8,128)(2,1)S(1)} %collective-permute-done.1.refs_2_), channel_id=1, source_target_pairs={{0,2},{2,0},{4,6},{6,4},{8,10},{10,8},{12,14},{14,12},{16,18},{18,... | collective-permute-start | bytes 537608 | tf_op jit(solution)/shard_map/ppermute | solution.py:44
  61.2 20.8 %collective-permute-start.33 = (bf16[120,1792]{1,0:T(8,128)(2,1)S(1)}, bf16[120,1792]{1,0:T(8,128)(2,1)S(1)}, u32[]{:S(2)}, u32[]{:S(2)}) collective-permute-start(bf16[120,1792]{1,0:T(8,128)(2,1)S(1)} %collective-permute-done.30), channel_id=1, source_target_pairs={{8,12},{10,14},{12,8},{14,10},{16,20},{18,22},{20,16},{22,18},{9,1... | collective-permute-start | bytes 1290248 | tf_op jit(solution)/shard_map/ppermute | solution.py:44
  71.3 18.4 %collective-permute-start.34 = (bf16[120,1792]{1,0:T(8,128)(2,1)S(1)}, bf16[120,1792]{1,0:T(8,128)(2,1)S(1)}, u32[]{:S(2)}, u32[]{:S(2)}) collective-permute-start(bf16[120,1792]{1,0:T(8,128)(2,1)S(1)} %collective-permute-done.31), channel_id=1, source_target_pairs={{0,4},{2,6},{4,0},{6,2},{24,28},{26,30},{28,24},{30,26},{1,5},{3,7... | collective-permute-start | bytes 1290248 | tf_op jit(solution)/shard_map/ppermute | solution.py:44
  74.7 33.5 %copy-start.2 = (bf16[8,77,1600]{2,0,1:T(8,128)(2,1)S(1)}, bf16[8,77,1600]{2,0,1:T(8,128)(2,1)}, u32[]{:S(2)}) copy-start(bf16[8,77,1600]{2,0,1:T(8,128)(2,1)} %param.15) | copy-start | bytes 5913604
  74.8 19.0 %collective-permute-start.10 = (bf16[100,896]{1,0:T(8,128)(2,1)S(1)}, bf16[100,896]{1,0:T(8,128)(2,1)S(1)}, u32[]{:S(2)}, u32[]{:S(2)}) collective-permute-start(bf16[100,896]{1,0:T(8,128)(2,1)S(1)} %broadcast_select_fusion.5.refs_8_), channel_id=1, source_target_pairs={{0,4},{2,6},{4,0},{6,2},{8,12},{10,14},{12,8},{14,10},{16,20},{18,... | collective-permute-start | bytes 537608 | tf_op jit(solution)/shard_map/ppermute | solution.py:44
  80.5 22.2 %collective-permute-start.22 = (bf16[120,1792]{1,0:T(8,128)(2,1)S(1)}, bf16[120,1792]{1,0:T(8,128)(2,1)S(1)}, u32[]{:S(2)}, u32[]{:S(2)}) collective-permute-start(bf16[120,1792]{1,0:T(8,128)(2,1)S(1)} %collective-permute-done.20.refs_4_), channel_id=1, source_target_pairs={{0,4},{2,6},{4,0},{6,2},{8,12},{10,14},{12,8},{14,10},{16,20},{18,... | collective-permute-start | bytes 1290248 | tf_op jit(solution)/shard_map/ppermute | solution.py:44
  82.0 22.7 %collective-permute-start.21 = (bf16[120,1792]{1,0:T(8,128)(2,1)S(1)}, bf16[120,1792]{1,0:T(8,128)(2,1)S(1)}, u32[]{:S(2)}, u32[]{:S(2)}) collective-permute-start(bf16[120,1792]{1,0:T(8,128)(2,1)S(1)} %collective-permute-done.20.refs_4_), channel_id=1, source_target_pairs={{0,2},{2,0},{4,6},{6,4},{8,10},{10,8},{12,14},{14,12},{16,18},{18,... | collective-permute-start | bytes 1290248 | tf_op jit(solution)/shard_map/ppermute | solution.py:44
  82.0 23.3 %collective-permute-start.19 = (bf16[120,1792]{1,0:T(8,128)(2,1)S(1)}, bf16[120,1792]{1,0:T(8,128)(2,1)S(1)}, u32[]{:S(2)}, u32[]{:S(2)}) collective-permute-start(bf16[120,1792]{1,0:T(8,128)(2,1)S(1)} %collective-permute-done.18.refs_2_), channel_id=1, source_target_pairs={{0,2},{2,0},{4,6},{6,4},{8,10},{10,8},{12,14},{14,12},{16,18},{18,... | collective-permute-start | bytes 1290248 | tf_op jit(solution)/shard_map/ppermute | solution.py:44
  89.7 15.0 %collective-permute-start.15 = (bf16[100,896]{1,0:T(8,128)(2,1)S(1)}, bf16[100,896]{1,0:T(8,128)(2,1)S(1)}, u32[]{:S(2)}, u32[]{:S(2)}) collective-permute-start(bf16[100,896]{1,0:T(8,128)(2,1)S(1)} %broadcast_select_fusion.4.refs_12_), channel_id=1, source_target_pairs={{0,4},{2,6},{4,0},{6,2},{8,12},{10,14},{12,8},{14,10},{16,20},{18,... | collective-permute-start | bytes 537608 | tf_op jit(solution)/shard_map/ppermute | solution.py:44
  93.7 13.0 %collective-permute-start.26 = (bf16[120,1792]{1,0:T(8,128)(2,1)S(1)}, bf16[120,1792]{1,0:T(8,128)(2,1)S(1)}, u32[]{:S(2)}, u32[]{:S(2)}) collective-permute-start(bf16[120,1792]{1,0:T(8,128)(2,1)S(1)} %broadcast_select_fusion.3.refs_8_), channel_id=1, source_target_pairs={{0,2},{2,0},{4,6},{6,4},{8,10},{10,8},{12,14},{14,12},{16,18},{18,... | collective-permute-start | bytes 1290248 | tf_op jit(solution)/shard_map/ppermute | solution.py:44
  102.7 4.4 %collective-permute-start.23 = (bf16[120,1792]{1,0:T(8,128)(2,1)S(1)}, bf16[120,1792]{1,0:T(8,128)(2,1)S(1)}, u32[]{:S(2)}, u32[]{:S(2)}) collective-permute-start(bf16[120,1792]{1,0:T(8,128)(2,1)S(1)} %collective-permute-done.22.refs_6_), channel_id=1, source_target_pairs={{0,2},{2,0},{4,6},{6,4},{8,10},{10,8},{12,14},{14,12},{16,18},{18,... | collective-permute-start | bytes 1290248 | tf_op jit(solution)/shard_map/ppermute | solution.py:44
  104.7 2.5 %collective-permute-start.29 = (bf16[120,1792]{1,0:T(8,128)(2,1)S(1)}, bf16[120,1792]{1,0:T(8,128)(2,1)S(1)}, u32[]{:S(2)}, u32[]{:S(2)}) collective-permute-start(bf16[120,1792]{1,0:T(8,128)(2,1)S(1)} %broadcast_select_fusion.2.refs_10_), channel_id=1, source_target_pairs={{0,2},{2,0},{4,6},{6,4},{8,10},{10,8},{12,14},{14,12},{16,18},{18,... | collective-permute-start | bytes 1290248 | tf_op jit(solution)/shard_map/ppermute | solution.py:44
  104.7 3.0 %collective-permute-start.32 = (bf16[120,1792]{1,0:T(8,128)(2,1)S(1)}, bf16[120,1792]{1,0:T(8,128)(2,1)S(1)}, u32[]{:S(2)}, u32[]{:S(2)}) collective-permute-start(bf16[120,1792]{1,0:T(8,128)(2,1)S(1)} %broadcast_select_fusion.1.refs_12_), channel_id=1, source_target_pairs={{0,2},{2,0},{4,6},{6,4},{8,10},{10,8},{12,14},{14,12},{16,18},{18,... | collective-permute-start | bytes 1290248 | tf_op jit(solution)/shard_map/ppermute | solution.py:44
  105.3 2.5 %collective-permute-start.35 = (bf16[120,1792]{1,0:T(8,128)(2,1)S(1)}, bf16[120,1792]{1,0:T(8,128)(2,1)S(1)}, u32[]{:S(2)}, u32[]{:S(2)}) collective-permute-start(bf16[120,1792]{1,0:T(8,128)(2,1)S(1)} %broadcast_select_fusion.refs_14_), channel_id=1, source_target_pairs={{0,2},{2,0},{4,6},{6,4},{8,10},{10,8},{12,14},{14,12},{16,18},{18,... | collective-permute-start | bytes 1290248 | tf_op jit(solution)/shard_map/ppermute | solution.py:44
  106.7 6.9 %collective-permute-start.9 = (bf16[100,896]{1,0:T(8,128)(2,1)S(1)}, bf16[100,896]{1,0:T(8,128)(2,1)S(1)}, u32[]{:S(2)}, u32[]{:S(2)}) collective-permute-start(bf16[100,896]{1,0:T(8,128)(2,1)S(1)} %broadcast_select_fusion.5.refs_8_), channel_id=1, source_target_pairs={{0,2},{2,0},{4,6},{6,4},{8,10},{10,8},{12,14},{14,12},{16,18},{18,... | collective-permute-start | bytes 537608 | tf_op jit(solution)/shard_map/ppermute | solution.py:44
  107.2 6.4 %collective-permute-start.6 = (bf16[100,896]{1,0:T(8,128)(2,1)S(1)}, bf16[100,896]{1,0:T(8,128)(2,1)S(1)}, u32[]{:S(2)}, u32[]{:S(2)}) collective-permute-start(bf16[100,896]{1,0:T(8,128)(2,1)S(1)} %collective-permute-done.5.refs_6_), channel_id=1, source_target_pairs={{0,2},{2,0},{4,6},{6,4},{8,10},{10,8},{12,14},{14,12},{16,18},{18,... | collective-permute-start | bytes 537608 | tf_op jit(solution)/shard_map/ppermute | solution.py:44
  107.3 6.3 %collective-permute-start.14 = (bf16[100,896]{1,0:T(8,128)(2,1)S(1)}, bf16[100,896]{1,0:T(8,128)(2,1)S(1)}, u32[]{:S(2)}, u32[]{:S(2)}) collective-permute-start(bf16[100,896]{1,0:T(8,128)(2,1)S(1)} %broadcast_select_fusion.4.refs_12_), channel_id=1, source_target_pairs={{0,2},{2,0},{4,6},{6,4},{8,10},{10,8},{12,14},{14,12},{16,18},{18,... | collective-permute-start | bytes 537608 | tf_op jit(solution)/shard_map/ppermute | solution.py:44
  107.7 5.9 %collective-permute-start.11 = (bf16[100,896]{1,0:T(8,128)(2,1)S(1)}, bf16[100,896]{1,0:T(8,128)(2,1)S(1)}, u32[]{:S(2)}, u32[]{:S(2)}) collective-permute-start(bf16[100,896]{1,0:T(8,128)(2,1)S(1)} %collective-permute-done.10.refs_10_), channel_id=1, source_target_pairs={{0,2},{2,0},{4,6},{6,4},{8,10},{10,8},{12,14},{14,12},{16,18},{18,... | collective-permute-start | bytes 537608 | tf_op jit(solution)/shard_map/ppermute | solution.py:44
  107.8 5.8 %collective-permute-start.16 = (bf16[100,896]{1,0:T(8,128)(2,1)S(1)}, bf16[100,896]{1,0:T(8,128)(2,1)S(1)}, u32[]{:S(2)}, u32[]{:S(2)}) collective-permute-start(bf16[100,896]{1,0:T(8,128)(2,1)S(1)} %collective-permute-done.15.refs_14_), channel_id=1, source_target_pairs={{0,2},{2,0},{4,6},{6,4},{8,10},{10,8},{12,14},{14,12},{16,18},{18,... | collective-permute-start | bytes 537608 | tf_op jit(solution)/shard_map/ppermute | solution.py:44
  108.2 5.4 %copy-start.4 = (s32[8]{0:T(128)S(1)}, s32[8]{0:T(128)}, u32[]{:S(2)}) copy-start(s32[8]{0:T(128)} %refs_16_.1) | copy-start | bytes 100
  112.1 1.4 %copy-start.5 = (f32[7,640,128]{2,1,0:T(8,128)}, f32[7,640,128]{2,1,0:T(8,128)S(1)}, u32[]{:S(2)}) copy-start(f32[7,640,128]{2,1,0:T(8,128)S(1)} %get-tuple-element.14.refs_18_) | copy-start | bytes 6881284
  113.6 1.6 %copy-start.6 = (f32[7,640,128]{2,1,0:T(8,128)S(1)}, f32[7,640,128]{2,1,0:T(8,128)}, u32[]{:S(2)}) copy-start(f32[7,640,128]{2,1,0:T(8,128)} %copy-done.5) | copy-start | bytes 6881284
  129.0 8.4 %collective-permute-start.37 = (bf16[8,16,1024]{2,1,0:T(8,128)(2,1)S(1)}, bf16[8,16,1024]{2,1,0:T(8,128)(2,1)S(1)}, u32[]{:S(2)}, u32[]{:S(2)}) collective-permute-start(bf16[8,16,1024]{2,1,0:T(8,128)(2,1)S(1)} %bitcast.37), channel_id=1, source_target_pairs={{0,1},{1,0},{2,3},{3,2},{4,5},{5,4},{6,7},{7,6},{8,9},{9,8},{10,11... | collective-permute-start | bytes 786440 | tf_op jit(solution)/shard_map/ppermute | solution.py:370
  137.4 0.8 copy-start.7
